TPU v7x, 256 devices: a whole 4x4x8 slice. The times are simulated.
256 devices in a mesh: seq: 32 (over z, y_hi, core), tp: 8 (over x, y_lo).
Axes of the slice: x: 4, y: 4 (y_hi: 2, y_lo: 2; y = y_hi * 2 + y_lo), z: 8, core: 2. Of those that a mesh axis runs over, the one named last changes fastest.
Arguments:
- stream: bfloat16 [8192, 2048], P('seq', 'tp'), may hold values from -16 to 16
- frames: int32 [8192], P('seq'), may hold values from 0 to 63, never falling along the last dimension, each value on 1 to 256 neighbouring positions
- fidelity: int32 [8192, 1], P('seq'), may hold values from 0 to 15; in each aligned block of 256 rows (0 to 255, 256 to 511, ...) at most 32 rows name the same one
- w_query: bfloat16 [2048, 2048], P(None, 'tp'), may hold values from -2 to 2
- w_key: bfloat16 [2048, 2048], P(None, 'tp'), may hold values from -2 to 2
- w_value: bfloat16 [2048, 2048], P(None, 'tp'), may hold values from -0.125 to 0.125
- w_output: bfloat16 [2048, 2048], P('tp'), may hold values from -0.125 to 0.125
- norm_gain: float32 [2048], replicated, may hold values from 0.1 to 1.9
- expert_gate: bfloat16 [32, 2048, 2816], P('seq', None, 'tp'), may hold values from -0.125 to 0.125
- expert_up: bfloat16 [32, 2048, 2816], P('seq', None, 'tp'), may hold values from -0.125 to 0.125
- expert_down: bfloat16 [32, 2816, 2048], P('seq', 'tp'), may hold values from -0.078125 to 0.078125
Outputs:
- result: bfloat16 [8192, 2048], P('seq', 'tp')
Inputs may be any that keep to these rules, and one draw needn't show every extreme that they name: `frames`: frame numbers never fall along the tokens; a frame holds 1 to 256 tokens, one exactly 256. `fidelity`: among the tokens of one index of seq (aligned blocks of 256 rows) no expert is named more than 32 times, a bound that some block reaches; every expert is named by some token.
All inputs are finite; a program needn't handle non-finite values.
Results may differ from a plain program's by a relative error of at most 0.02.
Values may be sent and summed in bfloat16 or wider, within the bound.
No kernel may reach another device: no remote copies, remote signals or barrier semaphores. Data moves between devices by JAX's collectives and lax.ppermute only.
A program may use at most 128 MiB of HBM per device.

v0:
```python
import math

import jax
import jax.numpy as jnp
from jax import lax
from jax.sharding import PartitionSpec as P

HEAD = 128
EXPERTS = 16
CAP = 32


big_negative = -1e30
norm_eps = 1e-05


def slot_rows(route_ids, tok_rows):
    onehot = (route_ids[:, None] == jnp.arange(EXPERTS, dtype=jnp.int32)[None, :]).astype(jnp.int32)
    places = jnp.sum(onehot * (jnp.cumsum(onehot, axis=0) - 1), axis=1)
    flat_slot = route_ids * CAP + places
    owner_table = (
        jnp.full((EXPERTS * CAP,), tok_rows, jnp.int32)
        .at[flat_slot]
        .set(jnp.arange(tok_rows, dtype=jnp.int32))
    )
    return (flat_slot, owner_table)


def shards(
    stream,
    frames,
    fidelity,
    w_query,
    w_key,
    w_value,
    w_output,
    norm_gain,
    expert_gate,
    expert_up,
    expert_down,
):
    tok_rows, slice_width = stream.shape
    tp_count = lax.axis_size("tp")
    seq_count = lax.axis_size("seq")
    width = slice_width * tp_count
    head_cols = w_query.shape[1]
    heads_here = head_cols // HEAD
    replicas = seq_count // EXPERTS
    col_start = lax.axis_index("tp") * slice_width
    gathered_rows = lax.all_gather(stream, "tp", axis=1, tiled=True)
    query_rows = jnp.dot(gathered_rows, w_query, preferred_element_type=jnp.float32).astype(
        jnp.bfloat16
    )
    key_rows = jnp.dot(gathered_rows, w_key, preferred_element_type=jnp.float32).astype(
        jnp.bfloat16
    )
    value_rows = jnp.dot(gathered_rows, w_value, preferred_element_type=jnp.float32).astype(
        jnp.bfloat16
    )
    query_heads = query_rows.reshape(tok_rows, heads_here, HEAD)
    score_scale = 1.0 / math.sqrt(HEAD)
    top_frame = jnp.max(frames)
    initial = (
        jnp.full((heads_here, tok_rows), big_negative, jnp.float32),
        jnp.zeros((heads_here, tok_rows), jnp.float32),
        jnp.zeros((tok_rows, heads_here, HEAD), jnp.float32),
    )
    key_piece = lax.all_gather(key_rows, "seq", axis=0, tiled=True)
    value_piece = lax.all_gather(value_rows, "seq", axis=0, tiled=True)
    frame_piece = lax.all_gather(frames, "seq", axis=0, tiled=True)

    def update(state):
        run_max, run_total, run_acc = state
        key_heads = key_piece.reshape(key_piece.shape[0], heads_here, HEAD)
        value_heads = value_piece.reshape(value_piece.shape[0], heads_here, HEAD)
        scores = (
            jnp.einsum("qhd,khd->hqk", query_heads, key_heads, preferred_element_type=jnp.float32)
            * score_scale
        )
        allowed = frame_piece[None, None, :] <= frames[None, :, None]
        scores = jnp.where(allowed, scores, big_negative)
        new_max = jnp.maximum(run_max, jnp.max(scores, axis=2))
        weights = jnp.where(allowed, jnp.exp(scores - new_max[:, :, None]), 0.0)
        new_total = jnp.sum(weights, axis=2)
        product = jnp.einsum(
            "hqk,khd->qhd",
            weights.astype(jnp.bfloat16),
            value_heads,
            preferred_element_type=jnp.float32,
        )
        return (new_max, new_total, product)

    run_max, run_total, run_acc = lax.cond(
        jnp.min(frame_piece) > top_frame, lambda unchanged: unchanged, update, initial
    )
    attended = (
        (run_acc / jnp.transpose(run_total)[:, :, None])
        .reshape(tok_rows, head_cols)
        .astype(jnp.bfloat16)
    )
    projected = jnp.dot(attended, w_output, preferred_element_type=jnp.float32)
    summed = lax.psum(projected.astype(jnp.bfloat16), "tp").astype(jnp.float32)
    mixed_full = (gathered_rows.astype(jnp.float32) + summed).astype(jnp.bfloat16)
    mixed_float = mixed_full.astype(jnp.float32)
    normed_full = (
        mixed_float
        * lax.rsqrt(jnp.mean(mixed_float * mixed_float, axis=1, keepdims=True) + norm_eps)
        * norm_gain[None, :]
    ).astype(jnp.bfloat16)
    mixed_rows = lax.dynamic_slice_in_dim(mixed_full, col_start, slice_width, 1)
    route_ids = fidelity[:, 0]
    flat_slot, owner_table = slot_rows(route_ids, tok_rows)
    padded = jnp.concatenate(
        [normed_full, jnp.zeros((1, normed_full.shape[1]), jnp.bfloat16)], axis=0
    )
    per_expert = jnp.take(padded, owner_table, axis=0).reshape(EXPERTS, CAP, normed_full.shape[1])
    sending = jnp.repeat(per_expert, replicas, axis=0)
    arrived = lax.all_to_all(sending, "seq", split_axis=0, concat_axis=0, tiled=True)
    flat_rows = arrived.reshape(-1, width)
    gate_act = jnp.dot(flat_rows, expert_gate[0], preferred_element_type=jnp.float32)
    up_act = jnp.dot(flat_rows, expert_up[0], preferred_element_type=jnp.float32)
    hidden = (jax.nn.silu(gate_act) * up_act).astype(jnp.bfloat16)
    lowered = jnp.dot(hidden, expert_down[0], preferred_element_type=jnp.float32).reshape(
        arrived.shape[0], arrived.shape[1], width
    )
    results = lax.psum(lowered.astype(jnp.bfloat16), "tp")
    returned = lax.all_to_all(results, "seq", split_axis=0, concat_axis=0, tiled=True)
    out_width = returned.shape[2]
    combined = jnp.sum(
        returned.astype(jnp.float32).reshape(EXPERTS, replicas, CAP, out_width), axis=1
    ).reshape(EXPERTS * CAP, out_width)
    own_rows = jnp.take(combined, flat_slot, axis=0)
    own_rows = lax.dynamic_slice_in_dim(own_rows, col_start, slice_width, 1)
    return (mixed_rows.astype(jnp.float32) + own_rows).astype(jnp.bfloat16)


def solution(mesh):
    return jax.shard_map(
        shards,
        mesh=mesh,
        in_specs=(
            P("seq", "tp"),
            P("seq"),
            P("seq", None),
            P(None, "tp"),
            P(None, "tp"),
            P(None, "tp"),
            P("tp", None),
            P(),
            P("seq", None, "tp"),
            P("seq", None, "tp"),
            P("seq", "tp", None),
        ),
        out_specs=P("seq", "tp"),
        check_vma=False,
    )
```

profile of v0, /device:TPU:6, one launch (start us, length us, event | category | flops | bytes accessed | tf_op | source)
XLA Modules:
  0.0 784.6 jit_solution(12655478996595157357)
XLA Ops:
  7.3 46.8 %all-gather.5.cloned.1.call-done = bf16[256,2048]{1,0:T(8,128)(2,1)} async-done(((bf16[256,256]{1,0:T(8,128)(2,1)}), bf16[256,2048]{1,0:T(8,128)(2,1)}) %all-gather.5.cloned.1.call-update) | async-done | bytes 1048592 | tf_op jit(solution)/shard_map/all_gather | solution.py:50
  54.1 2.7 convolution_convert_fusion.3
  56.9 2.6 convolution_convert_fusion.2
  60.2 43.5 %all-gather = s32[32,1,256]{2,1,0:T(1,128)} all-gather(s32[1,1,256]{2,1,0:T(1,128)S(1)} %bitcast.91), channel_id=1, replica_groups=mesh['seq'=32,'tp'=8] {'seq'}, dimensions={0}, use_global_device_ids=true | all-gather | bytes 33792 | tf_op jit(solution)/shard_map/all_gather | solution.py:70
  107.5 41.1 %all-gather.7.cloned.1.call-done = bf16[8192,256]{1,0:T(8,128)(2,1)} async-done(((bf16[256,256]{1,0:T(8,128)(2,1)}), bf16[8192,256]{1,0:T(8,128)(2,1)}) %all-gather.7.cloned.1.call-update) | async-done | bytes 4194320 | tf_op jit(solution)/shard_map/all_gather | solution.py:68
  148.6 86.3 %all-gather.9.cloned.1.call-done = bf16[8192,256]{1,0:T(8,128)(2,1)} async-done(((bf16[256,256]{1,0:T(8,128)(2,1)}), bf16[8192,256]{1,0:T(8,128)(2,1)}) %all-gather.9.cloned.1.call-update) | async-done | bytes 4194320 | tf_op jit(solution)/shard_map/all_gather | solution.py:69
  234.9 36.7 %conditional.1 = (f32[2,256]{1,0:T(2,128)S(1)}, f32[256,2,128]{0,2,1:T(8,128)}) conditional(s32[]{:T(128)} %convert_element_type.58, (s32[8192]{0:T(1024)}, s32[256]{0:T(256)S(1)}, bf16[256,256]{1,0:T(8,128)(2,1)}, bf16[8192,256]{1,0:T(8,128)(2,1)}, bf16[8192,256]{1,0:T(8,128)(2,1)}) %tuple.33, () %tuple.14), branch_computations={%region_2.5_spmd, %region_5.6_spmd} | conditional | flops 2204106240 | bytes 143570000 | solution.py:93
  234.9 2.1 broadcast_compare_fusion
  237.0 12.8 %fusion = (f32[2,256]{1,0:T(2,128)S(1)}, f32[2,256,8192]{2,1,0:T(8,128)}) fusion(pred[256,8192]{1,0:T(8,128)(4,1)S(1)} %broadcast_compare_fusion, bf16[8192,256]{1,0:T(8,128)(2,1)} %get-tuple-element.19, bf16[256,256]{1,0:T(8,128)(2,1)} %get-tuple-element.18), kind=kOutput, calls=%fused_computation.5 | convolution fusion | flops 1086324224 | bytes 23201792 | tf_op jit(solution)/shard_map/cond/branch_0_fun/qhd,khd->hqk/dot_general | solution.py:77
  249.8 9.2 %fusion.2 = f32[2,256]{1,0:T(2,128)S(1)} fusion(f32[2,256,8192]{2,1,0:T(8,128)} %get-tuple-element.31, f32[2,256]{1,0:T(2,128)S(1)} %broadcast_maximum_fusion, pred[256,8192]{1,0:T(8,128)(4,1)} %copy-done.3), kind=kLoop, calls=%fused_computation.7 | loop fusion | flops 20971008 | bytes 18878464 | tf_op jit(solution)/shard_map/cond/branch_0_fun/reduce_sum | solution.py:84
  259.0 2.1 copy-done.1
  261.1 8.8 %fusion.11 = f32[256,2,128]{2,0,1:T(8,128)} fusion(f32[2,256,8192]{2,1,0:T(8,128)S(1)} %copy-done.1, f32[2,256]{1,0:T(2,128)S(1)} %broadcast_maximum_fusion, pred[256,8192]{1,0:T(8,128)(4,1)} %copy-done.3, bf16[8192,256]{1,0:T(8,128)(2,1)} %get-tuple-element.20), kind=kOutput, calls=%fused_computation.16 | convolution fusion | flops 1094713344 | bytes 23332864 | tf_op jit(solution)/shard_map/cond/branch_0_fun/hqk,khd->qhd/dot_general | solution.py:85
  269.8 1.8 copy.28
  277.2 75.4 %all-reduce.4.cloned.1.call-done = bf16[256,2048]{1,0:T(8,128)(2,1)} async-done(((bf16[256,2048]{1,0:T(8,128)(2,1)}), bf16[256,2048]{1,0:T(8,128)(2,1)}) %all-reduce.4.cloned.1.call-update) | async-done | bytes 1048592 | tf_op jit(solution)/shard_map/psum | solution.py:102
  355.8 3.3 gather_fusion
  359.2 1.8 broadcast_select_fusion
  361.6 106.0 %all_to_all.10 = bf16[32,32,2048]{2,1,0:T(8,128)(2,1)S(1)} all-to-all(bf16[32,32,2048]{2,1,0:T(8,128)(2,1)S(1)} %bitcast.84), channel_id=1, replica_groups=mesh['seq'=32,'tp'=8] {'seq'}, dimensions={0} | all-to-all | bytes 8388608 | tf_op jit(solution)/shard_map/all_to_all | solution.py:118
  469.3 1.8 fusion.28
  471.5 4.3 convolution_convert_fusion
  475.8 183.1 %all-reduce.6.cloned.1.call-done = bf16[32,32,2048]{2,1,0:T(8,128)(2,1)} async-done(((bf16[32,32,2048]{2,1,0:T(8,128)(2,1)}), bf16[32,32,2048]{2,1,0:T(8,128)(2,1)}) %all-reduce.6.cloned.1.call-update) | async-done | bytes 4194320 | tf_op jit(solution)/shard_map/psum | solution.py:126
  658.9 10.8 %all-to-all-start.1 = ((bf16[32,32,2048]{2,1,0:T(8,128)(2,1)}), bf16[32,32,2048]{2,1,0:T(8,128)(2,1)}, u32[]{:S(2)}, u32[]{:S(2)}) async-start(bf16[32,32,2048]{2,1,0:T(8,128)(2,1)} %all-reduce.6.cloned.1.call-done), calls=%async_computation.1 | async-start | bytes 8388608 | tf_op jit(solution)/shard_map/all_to_all | solution.py:127
  669.8 96.5 %all-to-all-done.1 = bf16[32,32,2048]{2,1,0:T(8,128)(2,1)} async-done(((bf16[32,32,2048]{2,1,0:T(8,128)(2,1)}), bf16[32,32,2048]{2,1,0:T(8,128)(2,1)}, u32[]{:S(2)}, u32[]{:S(2)}) %all-to-all-start.1) | async-done | bytes 4194336 | tf_op jit(solution)/shard_map/all_to_all | solution.py:127
  766.2 5.6 convert_reduce_fusion
  771.8 4.6 gather_fusion.1
  (63 shorter events, 17.1 us)
Async XLA Ops:
  6.5 465.0 %copy-start = (bf16[1,352,2048]{2,1,0:T(8,128)(2,1)S(1)}, bf16[1,352,2048]{2,1,0:T(8,128)(2,1)}, u32[]{:S(2)}) copy-start(bf16[1,352,2048]{2,1,0:T(8,128)(2,1)} %param.23) | copy-start | bytes 4325380
  6.5 53.0 %copy-start.7 = (s32[256]{0:T(256)S(1)}, s32[256]{0:T(256)}, u32[]{:S(2)}) copy-start(s32[256]{0:T(256)} %param.14) | copy-start | bytes 3076
  6.5 99.9 %copy-start.5 = (bf16[2048,256]{1,0:T(8,128)(2,1)S(1)}, bf16[2048,256]{1,0:T(8,128)(2,1)}, u32[]{:S(2)}) copy-start(bf16[2048,256]{1,0:T(8,128)(2,1)} %param.16) | copy-start | bytes 3145732
  6.5 47.5 %all-gather.5.cloned.1.call-start = ((), (), s32[]{:S(2)}) async-start(), calls=%async_computation.2 | async-start | bytes 1179648 | tf_op jit(solution)/shard_map/all_gather | solution.py:50
  7.3 141.3 %all-gather.7.cloned.1.call-start = ((), (), s32[]{:S(2)}) async-start(), calls=%async_computation.3 | async-start | bytes 4325376 | tf_op jit(solution)/shard_map/all_gather | solution.py:68
  54.1 52.4 %copy-start.2 = (bf16[256,2048]{1,0:T(8,128)(2,1)S(1)}, bf16[256,2048]{1,0:T(8,128)(2,1)}, u32[]{:S(2)}) copy-start(bf16[256,2048]{1,0:T(8,128)(2,1)} %all-gather.5.cloned.1.call-done) | copy-start | bytes 3145732
  56.8 178.1 %all-gather.9.cloned.1.call-start = ((), (), s32[]{:S(2)}) async-start(), calls=%async_computation.4 | async-start | bytes 4325376 | tf_op jit(solution)/shard_map/all_gather | solution.py:69
  59.5 293.1 %all-reduce.4.cloned.1.call-start = ((), (), s32[]{:S(2)}) async-start(), calls=%async_computation.5 | async-start | bytes 2097152 | tf_op jit(solution)/shard_map/psum | solution.py:102
  234.9 37.7 %copy-start.6 = (bf16[256,2048]{1,0:T(8,128)(2,1)S(1)}, bf16[256,2048]{1,0:T(8,128)(2,1)}, u32[]{:S(2)}) copy-start(bf16[256,2048]{1,0:T(8,128)(2,1)} %param.19) | copy-start | bytes 3145732
  234.9 39.3 %copy-start.8 = (s32[256,1]{0,1:T(1,128)S(1)}, s32[256,1]{0,1:T(1,128)}, u32[]{:S(2)}) copy-start(s32[256,1]{0,1:T(1,128)} %param.15) | copy-start | bytes 3076
  237.0 12.8 %copy-start.3 = (pred[256,8192]{1,0:T(8,128)(4,1)}, pred[256,8192]{1,0:T(8,128)(4,1)S(1)}, u32[]{:S(2)}) copy-start(pred[256,8192]{1,0:T(8,128)(4,1)S(1)} %broadcast_compare_fusion) | copy-start | bytes 6291460 | tf_op jit(solution)/shard_map/cond
  249.8 11.3 %copy-start.1 = (f32[2,256,8192]{2,1,0:T(8,128)S(1)}, f32[2,256,8192]{2,1,0:T(8,128)}, u32[]{:S(2)}) copy-start(f32[2,256,8192]{2,1,0:T(8,128)} %get-tuple-element.31) | copy-start | bytes 50331652 | tf_op jit(solution)/shard_map/cond
  271.6 83.8 %copy-start.9 = (f32[2048]{0:T(1024)S(1)}, f32[2048]{0:T(1024)}, u32[]{:S(2)}) copy-start(f32[2048]{0:T(1024)} %param.20) | copy-start | bytes 24580
  274.2 384.8 %all-reduce.6.cloned.1.call-start = ((), (), s32[]{:S(2)}) async-start(), calls=%async_computation.6 | async-start | bytes 8388608 | tf_op jit(solution)/shard_map/psum | solution.py:126
  354.3 1.1 copy-start.4
  361.6 106.0 %copy-start.11 = (bf16[1,2048,352]{1,2,0:T(8,128)(2,1)S(1)}, bf16[1,2048,352]{1,2,0:T(8,128)(2,1)}, u32[]{:S(2)}) copy-start(bf16[1,2048,352]{1,2,0:T(8,128)(2,1)} %param.21) | copy-start | bytes 4325380
  467.6 1.8 copy-start.12
  658.9 107.3 %all-to-all-start.1 = ((bf16[32,32,2048]{2,1,0:T(8,128)(2,1)}), bf16[32,32,2048]{2,1,0:T(8,128)(2,1)}, u32[]{:S(2)}, u32[]{:S(2)}) async-start(bf16[32,32,2048]{2,1,0:T(8,128)(2,1)} %all-reduce.6.cloned.1.call-done), calls=%async_computation.1 | async-start | bytes 8388608 | tf_op jit(solution)/shard_map/all_to_all | solution.py:127
  771.8 4.6 copy-start.10
Sparse Core Ops, SparseCore 0:
  9.1 44.9 all-gather.4
  56.9 91.6 all-gather.6
  151.4 83.4 all-gather.8
  274.3 78.2 all-reduce.3
  475.9 182.9 all-reduce.5
where the time goes:
time: 786 us; the launch traced here: 785 us
  waiting for transfers between devices  530 us (67%)
  blocking collectives  149 us (19%)
  matrix products  37.3 us (5%)
  other arithmetic  26.8 us (3%)
  local copies, waits for them, and re-layouts  15.5 us (2%)
  between operations  14.6 us (2%)
  starting transfers between devices  11 us (1%)
    psum x1, waiting for transfers between devices, shards(): results = lax.psum(lowered.astype(jnp.bfloat16), 'tp')  183 us
    all_to_all x1, blocking collectives, shards(): lax.all_to_all(sending, 'seq', split_axis=0, concat_axis=0, tiled=True)  106 us
    all_to_all x1, waiting for transfers between devices, shards(): lax.all_to_all(results, 'seq', split_axis=0, concat_axis=0, tiled=True)  96.5 us
    all_gather x1, waiting for transfers between devices, shards(): value_piece = lax.all_gather(value_rows, 'seq', axis=0, tiled=True)  86.3 us
    psum x1, waiting for transfers between devices, shards(): summed = lax.psum(projected.astype(jnp.bfloat16), 'tp').astype(jnp.float32)  75.4 us
    all_gather x1, waiting for transfers between devices, shards(): gathered_rows = lax.all_gather(stream, 'tp', axis=1, tiled=True)  46.8 us
    all_gather x1, blocking collectives, shards(): frame_piece = lax.all_gather(frames, 'seq', axis=0, tiled=True)  43.5 us
    all_gather x1, waiting for transfers between devices, shards(): key_piece = lax.all_gather(key_rows, 'seq', axis=0, tiled=True)  41.1 us
  transfers between devices with their start and end apart: 6, of which 6 were waited for; matrix products, arithmetic and copies ran while one was open for 1% of the time, Pallas kernels for 0%

commit v1 on v0

v1 whole, which is shorter than its diff:
```python
import math

import jax
import jax.numpy as jnp
import numpy as np
from jax import lax
from jax.experimental import pallas as pl
from jax.experimental.pallas import tpu as pltpu
from jax.sharding import Mesh, PartitionSpec as P

HEAD = 128
EXPERTS = 16
CAP = 32
BLK = 256
NEG = -1e30
NORM_EPS = 1e-05
SEQ = ("z", "yh", "c")
CHIPS = ("z", "yh")
TP = ("x", "yl")
F32 = jnp.float32
BF16 = jnp.bfloat16

VMEM = pl.BlockSpec(memory_space=pltpu.VMEM)
SMEM = pl.BlockSpec(memory_space=pltpu.SMEM)


def nt_dot(a, b):
    return lax.dot_general(a, b, (((1,), (1,)), ((), ())), preferred_element_type=F32)


def tn_dot(a, b):
    return lax.dot_general(a, b, (((0,), (0,)), ((), ())), preferred_element_type=F32)


def qkv_kernel(info, *refs):
    blocks = refs[:8]
    wq, wk, wv, ends, kv_own, pack_c, q_own, pack_yc = refs[8:]
    first = info[8] == 0

    def project(w):
        total = None
        for j in range(8):
            rows = pl.ds(pl.multiple_of(info[j] * BLK, BLK), BLK)
            term = jnp.dot(blocks[j][...], w[rows, :], preferred_element_type=F32)
            total = term if total is None else total + term
        left, right = total[:, :HEAD], total[:, HEAD:]
        mine = jnp.where(first, left, right).astype(BF16)
        other = jnp.where(first, right, left).astype(BF16)
        return mine, other

    mine, other = project(wk)
    kv_own[:, :HEAD] = mine
    pack_c[:BLK, HEAD : 2 * HEAD] = other
    mine, other = project(wv)
    kv_own[:, HEAD:] = mine
    pack_c[:BLK, 2 * HEAD :] = other
    mine, other = project(wq)
    q_own[:BLK, :] = mine
    pack_c[:BLK, :HEAD] = other
    pack_yc[:BLK, :] = other
    tail = ends[...]
    q_own[BLK:, :] = tail
    pack_yc[BLK:, :] = tail
    pack_c[BLK:, :HEAD] = tail
    pack_c[BLK:, HEAD : 2 * HEAD] = tail
    pack_c[BLK:, 2 * HEAD :] = tail


def qkv(info, blocks, wq, wk, wv, ends):
    return pl.pallas_call(
        qkv_kernel,
        out_shape=(
            jax.ShapeDtypeStruct((BLK, 2 * HEAD), BF16),
            jax.ShapeDtypeStruct((BLK + 16, 3 * HEAD), BF16),
            jax.ShapeDtypeStruct((BLK + 16, HEAD), BF16),
            jax.ShapeDtypeStruct((BLK + 16, HEAD), BF16),
        ),
        in_specs=[SMEM] + [VMEM] * 12,
        out_specs=(VMEM,) * 4,
        cost_estimate=pl.CostEstimate(
            flops=2 * BLK * 2048 * 768, bytes_accessed=5 << 20, transcendentals=0
        ),
        name="qkv",
    )(info, *blocks, wq, wk, wv, ends)


def attend_kernel(info, q0, q1, q2, q3, kv, out, q_s, end_s, m_s, l_s, acc_s):
    z = info[0]
    scale = 1.0 / math.sqrt(HEAD)
    for g, q in enumerate((q0, q1, q2, q3)):
        cols = slice(g * BLK, (g + 1) * BLK)
        q_s[cols, :] = q[:BLK, :HEAD]
        for half in range(2):
            line = q[BLK + half : BLK + half + 1, :HEAD].astype(F32)
            lanes = slice(g * BLK + half * HEAD, g * BLK + (half + 1) * HEAD)
            end_s[:, lanes] = line.astype(jnp.int32) + BLK * (info[1 + g] + 1)
    m_s[...] = jnp.full_like(m_s, NEG)
    l_s[...] = jnp.zeros_like(l_s)
    acc_s[...] = jnp.zeros_like(acc_s)

    def visit(zk, masked):
        keys = kv[zk, :, :HEAD]
        values = kv[zk, :, HEAD:]
        for part in range(2):
            lanes = slice(part * 2 * BLK, (part + 1) * 2 * BLK)
            s = nt_dot(keys, q_s[lanes, :]) * scale
            old = m_s[:, lanes]
            if masked:
                row = lax.broadcasted_iota(jnp.int32, s.shape, 0)
                base = jnp.where(row < BLK, info[5] + 4 * zk, info[6] + 4 * zk - 1) * BLK
                ok = row + base < end_s[:, lanes]
                s = jnp.where(ok, s, NEG)
            top = jnp.maximum(old, jnp.max(s, axis=0, keepdims=True))
            p = jnp.exp(s - top)
            if masked:
                p = jnp.where(ok, p, 0.0)
            decay = jnp.exp(old - top)
            m_s[:, lanes] = top
            l_s[:, lanes] = l_s[:, lanes] * decay + jnp.sum(p, axis=0, keepdims=True)
            acc_s[:, lanes] = acc_s[:, lanes] * decay + tn_dot(values, p.astype(BF16))

    visit(z, True)

    def body(zk, carry):
        visit(zk, False)
        return carry

    lax.fori_loop(0, z, body, 0)

    @pl.when((z < 7) & (info[7] == 0))
    def _():
        visit(z + 1, True)

    for g in range(4):
        lanes = slice(g * BLK, (g + 1) * BLK)
        total = l_s[:, lanes]
        some = total > 0.0
        safe = jnp.where(some, total, 1.0)
        out[g, :HEAD, :] = acc_s[:, lanes] / safe
        lse = jnp.where(some, m_s[:, lanes] + jnp.log(safe), NEG)
        out[g, HEAD:, :] = jnp.broadcast_to(lse, (8, BLK))


def attend(info, q0, q1, q2, q3, kv):
    return pl.pallas_call(
        attend_kernel,
        out_shape=jax.ShapeDtypeStruct((4, HEAD + 8, BLK), F32),
        in_specs=[SMEM] + [VMEM] * 5,
        out_specs=VMEM,
        scratch_shapes=[
            pltpu.VMEM((4 * BLK, HEAD), BF16),
            pltpu.VMEM((1, 4 * BLK), jnp.int32),
            pltpu.VMEM((1, 4 * BLK), F32),
            pltpu.VMEM((1, 4 * BLK), F32),
            pltpu.VMEM((HEAD, 4 * BLK), F32),
        ],
        cost_estimate=pl.CostEstimate(
            flops=4 * 1024 * 4096 * HEAD, bytes_accessed=3 << 20, transcendentals=1024 * 4096
        ),
        name="attend",
    )(info, q0, q1, q2, q3, kv)


def merge_kernel(info, a0, a1, b0, b1, w, out):
    c = info[0]

    def merged(a, b):
        la, lb = a[HEAD : HEAD + 1, :], b[HEAD : HEAD + 1, :]
        top = jnp.maximum(la, lb)
        wa, wb = jnp.exp(la - top), jnp.exp(lb - top)
        inv = 1.0 / (wa + wb)
        return (a[:HEAD, :] * (wa * inv) + b[:HEAD, :] * (wb * inv)).astype(BF16)

    mine, other = merged(a0, a1), merged(b0, b1)
    rows_mine = pl.ds(pl.multiple_of(c * HEAD, HEAD), HEAD)
    rows_other = pl.ds(pl.multiple_of((1 - c) * HEAD, HEAD), HEAD)
    for t in range(8):
        cols = slice(t * BLK, (t + 1) * BLK)
        out[t] = (tn_dot(mine, w[rows_mine, cols]) + tn_dot(other, w[rows_other, cols])).astype(BF16)


def merge(info, a0, a1, b0, b1, w):
    return pl.pallas_call(
        merge_kernel,
        out_shape=jax.ShapeDtypeStruct((8, BLK, BLK), BF16),
        in_specs=[SMEM] + [VMEM] * 5,
        out_specs=VMEM,
        cost_estimate=pl.CostEstimate(
            flops=2 * BLK * BLK * 2048, bytes_accessed=3 << 20, transcendentals=1024
        ),
        name="merge",
    )(info, a0, a1, b0, b1, w)


def slots_kernel(parts, stream, slot, mixed, rows):
    total = stream[...].astype(F32) + jnp.sum(parts[...].astype(F32), axis=0)
    kept = total.astype(BF16)
    mixed[...] = kept
    ids = lax.broadcasted_iota(jnp.int32, (EXPERTS * CAP, BLK), 0)
    pick = jnp.where(ids == slot[...], 1.0, 0.0).astype(BF16)
    rows[...] = jnp.dot(pick, kept, preferred_element_type=F32).astype(BF16)


def to_slots(parts, stream, slot):
    return pl.pallas_call(
        slots_kernel,
        out_shape=(
            jax.ShapeDtypeStruct((BLK, BLK), BF16),
            jax.ShapeDtypeStruct((EXPERTS * CAP, BLK), BF16),
        ),
        in_specs=[VMEM] * 3,
        out_specs=(VMEM, VMEM),
        cost_estimate=pl.CostEstimate(
            flops=2 * 512 * BLK * BLK, bytes_accessed=2 << 20, transcendentals=0
        ),
        name="slots",
    )(parts, stream, slot)


def expert_kernel(x, gain, gate, up, down, out, n_s):
    square = None
    for t in range(8):
        v = x[0, t].astype(F32)
        term = jnp.sum(v * v, axis=1, keepdims=True)
        square = term if square is None else square + term
    inv = lax.rsqrt(square * (1.0 / 2048) + NORM_EPS)
    for t in range(8):
        cols = slice(t * BLK, (t + 1) * BLK)
        n_s[:, cols] = (x[0, t].astype(F32) * inv * gain[:, cols]).astype(BF16)
    g = nt_dot(n_s[...], gate[...])
    u = nt_dot(n_s[...], up[...])
    hidden = (g / (1.0 + jnp.exp(-g)) * u).astype(BF16)
    for t in range(8):
        cols = slice(t * BLK, (t + 1) * BLK)
        out[0, t] = jnp.dot(hidden, down[:, cols], preferred_element_type=F32).astype(BF16)


def expert(x, gain, gate, up, down):
    rows = 256
    units = gate.shape[0]
    whole = lambda i, j: (0, 0)
    return pl.pallas_call(
        expert_kernel,
        out_shape=jax.ShapeDtypeStruct(x.shape, BF16),
        grid=(2, x.shape[2] // rows),
        in_specs=[
            pl.BlockSpec((1, 8, rows, BLK), lambda i, j: (i, 0, j, 0)),
            pl.BlockSpec((1, 2048), whole),
            pl.BlockSpec((units, 2048), whole),
            pl.BlockSpec((units, 2048), whole),
            pl.BlockSpec((units, 2048), whole),
        ],
        out_specs=pl.BlockSpec((1, 8, rows, BLK), lambda i, j: (i, 0, j, 0)),
        scratch_shapes=[pltpu.VMEM((rows, 2048), BF16)],
        cost_estimate=pl.CostEstimate(
            flops=6 * 1024 * 2048 * units, bytes_accessed=13 << 20, transcendentals=1024 * units
        ),
        name="expert",
    )(x, gain, gate, up, down)


def finish_kernel(mixed, rows, slot, out):
    ids = lax.broadcasted_iota(jnp.int32, (EXPERTS * CAP, BLK), 0)
    pick = jnp.where(ids == slot[...], 1.0, 0.0).astype(BF16)
    out[...] = (mixed[...].astype(F32) + tn_dot(pick, rows[...])).astype(BF16)


def finish(mixed, rows, slot):
    return pl.pallas_call(
        finish_kernel,
        out_shape=jax.ShapeDtypeStruct((BLK, BLK), BF16),
        in_specs=[VMEM] * 3,
        out_specs=VMEM,
        cost_estimate=pl.CostEstimate(
            flops=2 * 512 * BLK * BLK, bytes_accessed=1 << 20, transcendentals=0
        ),
        name="finish",
    )(mixed, rows, slot)


def tp_shift(a, dx, dy):
    pairs = [(i * 2 + j, ((i + dx) % 4) * 2 + (j + dy) % 2) for i in range(4) for j in range(2)]
    return lax.ppermute(a, TP, pairs)


def swap(a, dy, dc):
    pairs = [(i * 2 + j, (i ^ dy) * 2 + (j ^ dc)) for i in range(2) for j in range(2)]
    return lax.ppermute(a, ("yh", "c"), pairs)


def shards(stream, frames, fidelity, wq, wk, wv, wo, gain, gate, up, down):
    z, yh, c = (lax.axis_index(a) for a in SEQ)
    x, yl = (lax.axis_index(a) for a in TP)

    shifts = [(dx, dy) for dx in range(4) for dy in range(2)]
    blocks = [stream if s == (0, 0) else tp_shift(stream, *s) for s in shifts]
    sources = [((x - dx) % 4) * 2 + (yl - dy) % 2 for dx, dy in shifts]

    follow = lax.ppermute(frames, SEQ, [((i + 1) % 32, i) for i in range(32)])
    last = (z == 7) & (yh == 1) & (c == 1)
    here = jnp.sum((frames[None, :] <= frames[:, None]).astype(jnp.int32), axis=1)
    after = jnp.sum((follow[None, :] <= frames[:, None]).astype(jnp.int32), axis=1)
    ends = here + jnp.where(last, 0, after) - BLK
    ends = jnp.pad(ends.reshape(2, HEAD), ((0, 14), (0, 0))).astype(BF16)

    route = fidelity[:, 0]
    spot = lax.iota(jnp.int32, BLK)
    same = (route[:, None] == route[None, :]) & (spot[None, :] < spot[:, None])
    slot = (route * CAP + jnp.sum(same.astype(jnp.int32), axis=1))[None, :]

    info = jnp.stack(sources + [c]).astype(jnp.int32)
    kv_own, pack_c, q_own, pack_yc = qkv(info, blocks, wq, wk, wv, ends)
    from_c = swap(pack_c, 0, 1)
    from_y = swap(q_own, 1, 0)
    from_yc = swap(pack_yc, 1, 1)
    kv = jnp.concatenate([kv_own, from_c[:BLK, HEAD:]], axis=0)
    kv = lax.all_gather(kv, "z", axis=0)

    block = lambda a, b: z * 4 + a * 2 + b
    info = jnp.stack(
        [z, block(yh, c), block(yh, 1 - c), block(1 - yh, c), block(1 - yh, 1 - c), yh * 2 + c, yh * 2 + 1 - c, yh]
    ).astype(jnp.int32)
    partial = attend(info, q_own, from_c, from_y, from_yc, kv)
    b0 = swap(partial[1], 0, 1)
    a1 = swap(partial[2], 1, 0)
    b1 = swap(partial[3], 1, 1)
    projected = merge(c.astype(jnp.int32)[None], partial[0], a1, b0, b1, wo)
    parts = lax.all_to_all(projected, TP, 0, 0, tiled=True)
    mixed, rows = to_slots(parts, stream, slot)

    sent = lax.all_to_all(rows.reshape(EXPERTS, CAP, BLK), CHIPS, 0, 0, tiled=True)
    full = lax.all_gather(sent.reshape(EXPERTS * CAP, BLK), ("c",) + TP, axis=0)
    full = full.reshape(2, 8, EXPERTS * CAP, BLK)
    lowered = expert(full, gain[None, :], gate[0].T, up[0].T, down[0])
    kept = lax.dynamic_index_in_dim(lowered, c, 0, keepdims=False)
    given = lax.dynamic_index_in_dim(lowered, 1 - c, 0, keepdims=False)
    taken = lax.ppermute(given, "c", [(0, 1), (1, 0)])
    pair = (kept.astype(F32) + taken.astype(F32)).astype(BF16)
    pieces = lax.all_to_all(pair, TP, 0, 0, tiled=True)
    summed = jnp.sum(pieces.astype(F32), axis=0).astype(BF16)
    back = lax.all_to_all(summed.reshape(EXPERTS, CAP, BLK), CHIPS, 0, 0, tiled=True)
    return finish(mixed, back.reshape(EXPERTS * CAP, BLK), slot)


def solution(mesh):
    axes = ("z", "yh", "c", "x", "yl")
    fine = Mesh(np.asarray(mesh.devices).reshape(8, 2, 2, 4, 2), axes)
    return jax.shard_map(
        shards,
        mesh=fine,
        in_specs=(
            P(SEQ, TP),
            P(SEQ),
            P(SEQ, None),
            P(None, TP),
            P(None, TP),
            P(None, TP),
            P(TP, None),
            P(),
            P(SEQ, None, TP),
            P(SEQ, None, TP),
            P(SEQ, TP, None),
        ),
        out_specs=P(SEQ, TP),
        check_vma=False,
    )
```

time: 786 us -> 266 us (0.34)
  waiting for transfers between devices: 530 us -> 98.9 us
  blocking collectives: 149 us -> 76.5 us
  matrix products: 37.3 us -> 0 us
  Pallas kernels: 0 us -> 30.4 us
  other arithmetic: 26.8 us -> 5.9 us
  starting transfers between devices: 11 us -> 30.6 us
    psum x2 -> x0, waiting for transfers between devices: 259 us -> none  [the longest x1 183 us: shards(): results = lax.psum(lowered.astype(jnp.bfloat16), 'tp')]
    all_gather x3 -> x2, waiting for transfers between devices: 174 us -> 67.1 us  [the longest x1 34.4 us: shards(): full = lax.all_gather(sent.reshape(EXPERTS * CAP, BLK), ('c',) + TP, axis=0)]
    all_to_all x1, waiting for transfers between devices: 96.5 us -> 12.8 us  [shards(): parts = lax.all_to_all(projected, TP, 0, 0, tiled=True)]
    all_gather x1 -> x0, blocking collectives: 43.5 us -> none  [shards(): frame_piece = lax.all_gather(frames, 'seq', axis=0, tiled=True)]
    dot_general x9 -> x0, matrix products: 37.3 us -> none  [the longest x1 12.8 us: update(): jnp.einsum('qhd,khd->hqk', query_heads, key_heads, preferred_element_type...]
    pallas_call x0 -> x6, Pallas kernels: none -> 30.4 us  [the longest x1 12.4 us: expert(): pl.pallas_call(expert_kernel, out_shape=jax.ShapeDtypeStruct(x.shape, BF1...]
    all_to_all x1 -> x3, blocking collectives: 106 us -> 76.5 us  [the longest x1 29.9 us: shards(): pieces = lax.all_to_all(pair, TP, 0, 0, tiled=True)]
    ppermute x0 -> x15, starting transfers between devices: none -> 25.3 us  [the longest x7 11.1 us: tp_shift(): return lax.ppermute(a, TP, pairs)]
  transfers between devices with their start and end apart: 6 -> 18, of which waited for: 6 -> 12; matrix products, arithmetic and copies ran while one was open for 1% -> 1% of each run, Pallas kernels for 0% -> 0%
where the time goes in v1:
time: 266 us; the launch traced here: 265 us
  waiting for transfers between devices  98.9 us (37%)
  blocking collectives  76.5 us (29%)
  starting transfers between devices  30.6 us (12%)
  Pallas kernels  30.4 us (11%)
  between operations  13.5 us (5%)
  local copies, waits for them, and re-layouts  9.11 us (3%)
  other arithmetic  5.9 us (2%)
    all_gather x1, waiting for transfers between devices, shards(): full = lax.all_gather(sent.reshape(EXPERTS * CAP, BLK), ('c',) + TP, axis=0)  34.4 us
    all_gather x1, waiting for transfers between devices, shards(): kv = lax.all_gather(kv, 'z', axis=0)  32.7 us
    all_to_all x1, blocking collectives, shards(): pieces = lax.all_to_all(pair, TP, 0, 0, tiled=True)  29.9 us
    all_to_all x1, blocking collectives, shards(): lax.all_to_all(rows.reshape(EXPERTS, CAP, BLK), CHIPS, 0, 0, tiled=True)  24.9 us
    all_to_all x1, blocking collectives, shards(): lax.all_to_all(summed.reshape(EXPERTS, CAP, BLK), CHIPS, 0, 0, tiled=True)  21.7 us
    all_to_all x1, waiting for transfers between devices, shards(): parts = lax.all_to_all(projected, TP, 0, 0, tiled=True)  12.8 us
    pallas_call x1, Pallas kernels, expert(): pl.pallas_call(expert_kernel, out_shape=jax.ShapeDtypeStruct(x.shape, BF1...  12.4 us
    ppermute x7, starting transfers between devices, tp_shift(): return lax.ppermute(a, TP, pairs)  11.1 us
  transfers between devices with their start and end apart: 18, of which 12 were waited for; matrix products, arithmetic and copies ran while one was open for 1% of the time, Pallas kernels for 0%

profile of v1, /device:TPU:6, one launch (start us, length us, event | category | flops | bytes accessed | tf_op | source)
XLA Modules:
  0.0 264.9 jit_solution(3316143722350507156)
XLA Ops:
  8.9 3.2 %collective-permute-start.4 = (bf16[256,256]{1,0:T(8,128)(2,1)}, bf16[256,256]{1,0:T(8,128)(2,1)S(1)}, u32[]{:S(2)}, u32[]{:S(2)}) collective-permute-start(bf16[256,256]{1,0:T(8,128)(2,1)} %stream.1), channel_id=1, source_target_pairs={{0,5},{1,4},{2,7},{3,6},{4,1},{5,0},{6,3},{7,2},{8,13},{9,12},{10,... | collective-permute-start | bytes 393224 | tf_op jit(solution)/shard_map/ppermute | solution.py:283
  12.3 6.9 %collective-permute-start.7 = (s32[256]{0:T(256)}, s32[256]{0:T(256)S(1)}, u32[]{:S(2)}, u32[]{:S(2)}) collective-permute-start(s32[256]{0:T(256)} %param.12), channel_id=1, source_target_pairs={{8,0},{16,8},{24,16},{32,24},{40,32},{48,40},{56,48},{64,56},{72,6... | collective-permute-start | bytes 3080 | tf_op jit(solution)/shard_map/ppermute | solution.py:299
  20.7 2.7 %collective-permute-start.2 = (bf16[256,256]{1,0:T(8,128)(2,1)}, bf16[256,256]{1,0:T(8,128)(2,1)S(1)}, u32[]{:S(2)}, u32[]{:S(2)}) collective-permute-start(bf16[256,256]{1,0:T(8,128)(2,1)} %stream.1), channel_id=1, source_target_pairs={{0,3},{1,2},{2,5},{3,4},{4,7},{5,6},{6,1},{7,0},{8,11},{9,10},{10,... | collective-permute-start | bytes 393224 | tf_op jit(solution)/shard_map/ppermute | solution.py:283
  27.7 2.0 collective-permute-done.1.refs_2_
  31.6 4.1 %qkv.1 = (bf16[256,256]{1,0:T(8,128)(2,1)}, bf16[272,384]{1,0:T(8,128)(2,1)}, bf16[272,128]{1,0:T(8,128)(2,1)}, bf16[272,128]{1,0:T(8,128)(2,1)}) custom-call(s32[9]{0:T(128)} %stack.72.info, bf16[256,256]{1,0:T(8,128)(2,1)} %stream.1, bf16[256,256]{1,0:T(8,128)(2,1)} %copy-done.10, bf16[256,256]{1,0:T(8,128)(2,1)} %copy-done.9, bf16[256,256]{1,0:T(8,128)(2,1)} %copy-done.8, ...), custom_call_target="tpu_custom_call" | custom-call | flops 805306368 | bytes 5242880 | tf_op jit(solution)/shard_map/qkv/pallas_call | solution.py:70
  39.2 3.3 %collective-permute-start.9 = (bf16[272,128]{1,0:T(8,128)(2,1)}, bf16[272,128]{1,0:T(8,128)(2,1)S(1)}, u32[]{:S(2)}, u32[]{:S(2)}) collective-permute-start(bf16[272,128]{1,0:T(8,128)(2,1)} %get-tuple-element.11.q0), channel_id=1, source_target_pairs={{0,16},{8,24},{16,0},{24,8},{1,17},{9,25},{17,1},{25,9},{2,18},{10... | collective-permute-start | bytes 208904 | tf_op jit(solution)/shard_map/ppermute | solution.py:288
  43.1 2.0 collective-permute-done.10.q3
  46.9 32.7 %all-gather.6.cloned.1.call-done = bf16[4096,256]{1,0:T(8,128)(2,1)} async-done(((bf16[512,256]{1,0:T(8,128)(2,1)}), bf16[4096,256]{1,0:T(8,128)(2,1)}) %all-gather.6.cloned.1.call-update) | async-done | bytes 2097168 | tf_op jit(solution)/shard_map/all_gather | solution.py:317
  79.6 6.3 %attend.1 = f32[4,136,256]{2,1,0:T(8,128)} custom-call(s32[8]{0:T(128)} %stack.63.info, bf16[272,128]{1,0:T(8,128)(2,1)} %get-tuple-element.11.q0, bf16[272,384]{1,0:T(8,128)(2,1)} %copy-done.11, bf16[272,128]{1,0:T(8,128)(2,1)} %copy-done.14, bf16[272,128]{1,0:T(8,128)(2,1)} %copy-done.13, bf16[8,512,256]{2,1,0:T(8,128)(2,1)} %bitcast.57), custom_call_target="tpu_custom_call" | custom-call | flops 2147483648 | bytes 3145728 | tf_op jit(solution)/shard_map/attend/pallas_call | solution.py:145
  89.1 2.3 collective-permute-start.11
  91.4 2.3 collective-permute-done.13.b1
  93.8 3.0 %collective-permute-done.11.a1 = f32[136,256]{1,0:T(8,128)S(1)} collective-permute-done((f32[136,256]{1,0:T(8,128)S(1)}, f32[136,256]{1,0:T(8,128)S(1)}, u32[]{:S(2)}, u32[]{:S(2)}) %collective-permute-start.11) | collective-permute-done | bytes 139296 | tf_op jit(solution)/shard_map/ppermute | solution.py:288
  97.4 3.3 %merge.1 = bf16[8,256,256]{2,1,0:T(8,128)(2,1)} custom-call(s32[1]{0:T(128)} %bitcast.info, f32[136,256]{1,0:T(8,128)} %get-tuple-element.22.a0, f32[136,256]{1,0:T(8,128)} %copy-done.3, f32[136,256]{1,0:T(8,128)} %copy-done.2, f32[136,256]{1,0:T(8,128)} %copy-done.1, bf16[256,2048]{1,0:T(8,128)(2,1)} %w.1), custom_call_target="tpu_custom_call" | custom-call | flops 268435456 | bytes 3145728 | tf_op jit(solution)/shard_map/merge/pallas_call | solution.py:183
  100.7 5.3 %all-to-all-start = ((bf16[8,256,256]{2,1,0:T(8,128)(2,1)}), bf16[8,256,256]{2,1,0:T(8,128)(2,1)S(1)}, u32[]{:S(2)}, u32[]{:S(2)}) async-start(bf16[8,256,256]{2,1,0:T(8,128)(2,1)} %merge.1), calls=%async_computation | async-start | bytes 2097152 | tf_op jit(solution)/shard_map/all_to_all | solution.py:328
  106.7 12.8 %all-to-all-done.parts = bf16[8,256,256]{2,1,0:T(8,128)(2,1)S(1)} async-done(((bf16[8,256,256]{2,1,0:T(8,128)(2,1)}), bf16[8,256,256]{2,1,0:T(8,128)(2,1)S(1)}, u32[]{:S(2)}, u32[]{:S(2)}) %all-to-all-start) | async-done | bytes 1048608 | tf_op jit(solution)/shard_map/all_to_all | solution.py:328
  120.4 2.4 slots.1
  122.9 24.9 %all_to_all.20 = bf16[16,32,256]{2,1,0:T(8,128)(2,1)} all-to-all(bf16[16,32,256]{2,1,0:T(8,128)(2,1)} %bitcast.53), channel_id=1, replica_groups=mesh['z'=8,'yh'=2,'c'=2,'x'=4,'yl'=2] {'z','yh'}, dimensions={0} | all-to-all | bytes 524288 | tf_op jit(solution)/shard_map/all_to_all | solution.py:331
  147.8 34.4 %all-gather.4.cloned.1.call-done = bf16[16,512,256]{2,1,0:T(8,128)(2,1)} async-done(((bf16[1,512,256]{2,1,0:T(8,128)(2,1)}), bf16[16,512,256]{2,1,0:T(8,128)(2,1)}) %all-gather.4.cloned.1.call-update) | async-done | bytes 4194320 | tf_op jit(solution)/shard_map/all_gather | solution.py:332
  182.2 12.4 %expert.1 = bf16[2,8,512,256]{3,2,1,0:T(8,128)(2,1)} custom-call(bf16[2,8,512,256]{3,2,1,0:T(8,128)(2,1)} %bitcast.56, f32[1,2048]{1,0:T(1,128)} %bitcast.61, bf16[352,2048]{1,0:T(8,128)(2,1)} %bitcast.58, bf16[352,2048]{1,0:T(8,128)(2,1)} %bitcast.59, bf16[352,2048]{1,0:T(8,128)(2,1)} %bitcast.60), custom_call_target="tpu_custom_call" | custom-call | flops 4429185024 | bytes 13631488 | tf_op jit(solution)/shard_map/expert/pallas_call | solution.py:242
  194.6 3.1 %dynamic-slice_bitcast_fusion = bf16[8,512,256]{2,1,0:T(8,128)(2,1)} fusion(bf16[2,8,512,256]{3,2,1,0:T(8,128)(2,1)} %expert.1, s32[]{:T(128)S(6)} %select_n.73), kind=kLoop, calls=%fused_computation.2 | loop fusion | bytes 4194308 | tf_op jit(solution)/shard_map/jit(dynamic_index_in_dim)/squeeze | solution.py:336
  197.9 4.1 %collective-permute-done.14 = bf16[8,512,256]{2,1,0:T(8,128)(2,1)S(1)} collective-permute-done((bf16[8,512,256]{2,1,0:T(8,128)(2,1)}, bf16[8,512,256]{2,1,0:T(8,128)(2,1)S(1)}, u32[]{:S(2)}, u32[]{:S(2)}) %collective-permute-start.14) | collective-permute-done | bytes 2097184 | tf_op jit(solution)/shard_map/ppermute | solution.py:337
  202.0 2.1 fusion
  204.1 29.9 %all_to_all.21 = bf16[8,512,256]{2,1,0:T(8,128)(2,1)S(1)} all-to-all(bf16[8,512,256]{2,1,0:T(8,128)(2,1)S(1)} %fusion), channel_id=1, replica_groups=mesh['z'=8,'yh'=2,'c'=2,'x'=4,'yl'=2] {'x','yl'}, dimensions={0} | all-to-all | bytes 4194304 | tf_op jit(solution)/shard_map/all_to_all | solution.py:339
  234.4 21.7 %all_to_all.22 = bf16[16,32,256]{2,1,0:T(8,128)(2,1)} all-to-all(bf16[16,32,256]{2,1,0:T(8,128)(2,1)S(1)} %bitcast.50), channel_id=1, replica_groups=mesh['z'=8,'yh'=2,'c'=2,'x'=4,'yl'=2] {'z','yh'}, dimensions={0} | all-to-all | bytes 524288 | tf_op jit(solution)/shard_map/all_to_all | solution.py:341
  (66 shorter events, 24.2 us)
Async XLA Ops:
  6.5 73.1 %all-gather.6.cloned.1.call-start = ((), (), s32[]{:S(2)}) async-start(), calls=%async_computation.5 | async-start | bytes 2359296 | tf_op jit(solution)/shard_map/all_gather | solution.py:317
  6.5 17.9 %collective-permute-start.6 = (bf16[256,256]{1,0:T(8,128)(2,1)}, bf16[256,256]{1,0:T(8,128)(2,1)S(1)}, u32[]{:S(2)}, u32[]{:S(2)}) collective-permute-start(bf16[256,256]{1,0:T(8,128)(2,1)} %stream.1), channel_id=1, source_target_pairs={{0,7},{1,6},{2,1},{3,0},{4,3},{5,2},{6,5},{7,4},{8,15},{9,14},{10,... | collective-permute-start | bytes 393224 | tf_op jit(solution)/shard_map/ppermute | solution.py:283
  8.4 17.4 %collective-permute-start.5 = (bf16[256,256]{1,0:T(8,128)(2,1)}, bf16[256,256]{1,0:T(8,128)(2,1)S(1)}, u32[]{:S(2)}, u32[]{:S(2)}) collective-permute-start(bf16[256,256]{1,0:T(8,128)(2,1)} %stream.1), channel_id=1, source_target_pairs={{0,6},{1,7},{2,0},{3,1},{4,2},{5,3},{6,4},{7,5},{8,14},{9,15},{10,... | collective-permute-start | bytes 393224 | tf_op jit(solution)/shard_map/ppermute | solution.py:283
  8.9 18.8 %collective-permute-start.4 = (bf16[256,256]{1,0:T(8,128)(2,1)}, bf16[256,256]{1,0:T(8,128)(2,1)S(1)}, u32[]{:S(2)}, u32[]{:S(2)}) collective-permute-start(bf16[256,256]{1,0:T(8,128)(2,1)} %stream.1), channel_id=1, source_target_pairs={{0,5},{1,4},{2,7},{3,6},{4,1},{5,0},{6,3},{7,2},{8,13},{9,12},{10,... | collective-permute-start | bytes 393224 | tf_op jit(solution)/shard_map/ppermute | solution.py:283
  12.1 15.6 %collective-permute-start.3 = (bf16[256,256]{1,0:T(8,128)(2,1)}, bf16[256,256]{1,0:T(8,128)(2,1)S(1)}, u32[]{:S(2)}, u32[]{:S(2)}) collective-permute-start(bf16[256,256]{1,0:T(8,128)(2,1)} %stream.1), channel_id=1, source_target_pairs={{0,4},{1,5},{2,6},{3,7},{4,0},{5,1},{6,2},{7,3},{8,12},{9,13},{10,... | collective-permute-start | bytes 393224 | tf_op jit(solution)/shard_map/ppermute | solution.py:283
  12.3 8.4 %collective-permute-start.7 = (s32[256]{0:T(256)}, s32[256]{0:T(256)S(1)}, u32[]{:S(2)}, u32[]{:S(2)}) collective-permute-start(s32[256]{0:T(256)} %param.12), channel_id=1, source_target_pairs={{8,0},{16,8},{24,16},{32,24},{40,32},{48,40},{56,48},{64,56},{72,6... | collective-permute-start | bytes 3080 | tf_op jit(solution)/shard_map/ppermute | solution.py:299
  20.7 7.0 %collective-permute-start.2 = (bf16[256,256]{1,0:T(8,128)(2,1)}, bf16[256,256]{1,0:T(8,128)(2,1)S(1)}, u32[]{:S(2)}, u32[]{:S(2)}) collective-permute-start(bf16[256,256]{1,0:T(8,128)(2,1)} %stream.1), channel_id=1, source_target_pairs={{0,3},{1,2},{2,5},{3,4},{4,7},{5,6},{6,1},{7,0},{8,11},{9,10},{10,... | collective-permute-start | bytes 393224 | tf_op jit(solution)/shard_map/ppermute | solution.py:283
  24.5 6.5 %copy-start.4 = (bf16[256,256]{1,0:T(8,128)(2,1)}, bf16[256,256]{1,0:T(8,128)(2,1)S(1)}, u32[]{:S(2)}) copy-start(bf16[256,256]{1,0:T(8,128)(2,1)S(1)} %collective-permute-done.6.refs_7_) | copy-start | bytes 393220
  24.5 5.3 %collective-permute-start.1 = (bf16[256,256]{1,0:T(8,128)(2,1)}, bf16[256,256]{1,0:T(8,128)(2,1)S(1)}, u32[]{:S(2)}, u32[]{:S(2)}) collective-permute-start(bf16[256,256]{1,0:T(8,128)(2,1)} %stream.1), channel_id=1, source_target_pairs={{0,2},{1,3},{2,4},{3,5},{4,6},{5,7},{6,0},{7,1},{8,10},{9,11},{10,... | collective-permute-start | bytes 393224 | tf_op jit(solution)/shard_map/ppermute | solution.py:283
  25.7 5.2 %copy-start.5 = (bf16[256,256]{1,0:T(8,128)(2,1)}, bf16[256,256]{1,0:T(8,128)(2,1)S(1)}, u32[]{:S(2)}) copy-start(bf16[256,256]{1,0:T(8,128)(2,1)S(1)} %collective-permute-done.5.refs_6_) | copy-start | bytes 393220
  25.7 5.2 %collective-permute-start = (bf16[256,256]{1,0:T(8,128)(2,1)}, bf16[256,256]{1,0:T(8,128)(2,1)S(1)}, u32[]{:S(2)}, u32[]{:S(2)}) collective-permute-start(bf16[256,256]{1,0:T(8,128)(2,1)} %stream.1), channel_id=1, source_target_pairs={{0,1},{1,0},{2,3},{3,2},{4,5},{5,4},{6,7},{7,6},{8,9},{9,8},{10,11... | collective-permute-start | bytes 393224 | tf_op jit(solution)/shard_map/ppermute | solution.py:283
  35.7 1.7 collective-permute-start.8
  37.4 42.3 %copy-start.11 = (bf16[272,384]{1,0:T(8,128)(2,1)}, bf16[272,384]{1,0:T(8,128)(2,1)S(1)}, u32[]{:S(2)}) copy-start(bf16[272,384]{1,0:T(8,128)(2,1)S(1)} %collective-permute-done.8.q1) | copy-start | bytes 626692
  39.1 6.0 %collective-permute-start.10 = (bf16[272,128]{1,0:T(8,128)(2,1)}, bf16[272,128]{1,0:T(8,128)(2,1)S(1)}, u32[]{:S(2)}, u32[]{:S(2)}) collective-permute-start(bf16[272,128]{1,0:T(8,128)(2,1)} %get-tuple-element.13), channel_id=1, source_target_pairs={{0,24},{8,16},{16,8},{24,0},{1,25},{9,17},{17,9},{25,1},{2,26},{10... | collective-permute-start | bytes 208904 | tf_op jit(solution)/shard_map/ppermute | solution.py:288
  39.2 7.7 %collective-permute-start.9 = (bf16[272,128]{1,0:T(8,128)(2,1)}, bf16[272,128]{1,0:T(8,128)(2,1)S(1)}, u32[]{:S(2)}, u32[]{:S(2)}) collective-permute-start(bf16[272,128]{1,0:T(8,128)(2,1)} %get-tuple-element.11.q0), channel_id=1, source_target_pairs={{0,16},{8,24},{16,0},{24,8},{1,17},{9,25},{17,1},{25,9},{2,18},{10... | collective-permute-start | bytes 208904 | tf_op jit(solution)/shard_map/ppermute | solution.py:288
  45.1 34.5 %copy-start.13 = (bf16[272,128]{1,0:T(8,128)(2,1)}, bf16[272,128]{1,0:T(8,128)(2,1)S(1)}, u32[]{:S(2)}) copy-start(bf16[272,128]{1,0:T(8,128)(2,1)S(1)} %collective-permute-done.10.q3) | copy-start | bytes 208900
  46.9 32.7 %copy-start.14 = (bf16[272,128]{1,0:T(8,128)(2,1)}, bf16[272,128]{1,0:T(8,128)(2,1)S(1)}, u32[]{:S(2)}) copy-start(bf16[272,128]{1,0:T(8,128)(2,1)S(1)} %collective-permute-done.9.q2) | copy-start | bytes 208900
  87.8 6.0 %collective-permute-start.13 = (f32[136,256]{1,0:T(8,128)S(1)}, f32[136,256]{1,0:T(8,128)S(1)}, u32[]{:S(2)}, u32[]{:S(2)}) collective-permute-start(f32[136,256]{1,0:T(8,128)S(1)} %get-tuple-element.19), channel_id=1, source_target_pairs={{0,24},{8,16},{16,8},{24,0},{1,25},{9,17},{17,9},{25,1},{2,26},{10... | collective-permute-start | bytes 417800 | tf_op jit(solution)/shard_map/ppermute | solution.py:288
  87.8 6.0 %collective-permute-start.12 = (f32[136,256]{1,0:T(8,128)S(1)}, f32[136,256]{1,0:T(8,128)S(1)}, u32[]{:S(2)}, u32[]{:S(2)}) collective-permute-start(f32[136,256]{1,0:T(8,128)S(1)} %get-tuple-element.20), channel_id=1, source_target_pairs={{0,8},{8,0},{16,24},{24,16},{1,9},{9,1},{17,25},{25,17},{2,10},{10... | collective-permute-start | bytes 417800 | tf_op jit(solution)/shard_map/ppermute | solution.py:288
  89.1 7.6 %collective-permute-start.11 = (f32[136,256]{1,0:T(8,128)S(1)}, f32[136,256]{1,0:T(8,128)S(1)}, u32[]{:S(2)}, u32[]{:S(2)}) collective-permute-start(f32[136,256]{1,0:T(8,128)S(1)} %get-tuple-element.21), channel_id=1, source_target_pairs={{0,16},{8,24},{16,0},{24,8},{1,17},{9,25},{17,1},{25,9},{2,18},{10... | collective-permute-start | bytes 417800 | tf_op jit(solution)/shard_map/ppermute | solution.py:288
  97.4 8.5 %copy-start.12 = (s32[256,1]{0,1:T(1,128)S(1)}, s32[256,1]{0,1:T(1,128)}, u32[]{:S(2)}) copy-start(s32[256,1]{0,1:T(1,128)} %param.13) | copy-start | bytes 3076
  100.7 18.8 %all-to-all-start = ((bf16[8,256,256]{2,1,0:T(8,128)(2,1)}), bf16[8,256,256]{2,1,0:T(8,128)(2,1)S(1)}, u32[]{:S(2)}, u32[]{:S(2)}) async-start(bf16[8,256,256]{2,1,0:T(8,128)(2,1)} %merge.1), calls=%async_computation | async-start | bytes 2097152 | tf_op jit(solution)/shard_map/all_to_all | solution.py:328
  106.0 76.2 %all-gather.4.cloned.1.call-start = ((), (), s32[]{:S(2)}) async-start(), calls=%async_computation.4 | async-start | bytes 4456448 | tf_op jit(solution)/shard_map/all_gather | solution.py:332
  197.6 4.4 %collective-permute-start.14 = (bf16[8,512,256]{2,1,0:T(8,128)(2,1)}, bf16[8,512,256]{2,1,0:T(8,128)(2,1)S(1)}, u32[]{:S(2)}, u32[]{:S(2)}) collective-permute-start(bf16[8,512,256]{2,1,0:T(8,128)(2,1)} %dynamic-slice_bitcast_fusion), channel_id=1, source_target_pairs={{0,8},{8,0},{1,9},{9,1},{2,10},{10,2},{3,11},{11,3},{4,12},{12,4},... | collective-permute-start | bytes 6291464 | tf_op jit(solution)/shard_map/ppermute | solution.py:337
  (9 other events, 19.2 us)
Sparse Core Ops, SparseCore 0:
  39.2 40.3 all-gather.5
  147.9 34.2 all-gather.3

commit v2 on v1

v2 whole, which is shorter than its diff:
```python
import functools
import math

import jax
import jax.numpy as jnp
import numpy as np
from jax import lax
from jax.experimental import pallas as pl
from jax.experimental.pallas import tpu as pltpu
from jax.sharding import Mesh, PartitionSpec as P

HEAD = 128
EXPERTS = 16
CAP = 32
BLK = 256
NEG = -1e30
NORM_EPS = 1e-05
SEQ = ("z", "yh", "c")
CHIPS = ("z", "yh")
TP = ("x", "yl")
SHIFTS = [(dx, dy) for dx in range(4) for dy in range(2)]
F32 = jnp.float32
BF16 = jnp.bfloat16

VMEM = pl.BlockSpec(memory_space=pltpu.VMEM)
SMEM = pl.BlockSpec(memory_space=pltpu.SMEM)


def nt_dot(a, b):
    return lax.dot_general(a, b, (((1,), (1,)), ((), ())), preferred_element_type=F32)


def tn_dot(a, b):
    return lax.dot_general(a, b, (((0,), (0,)), ((), ())), preferred_element_type=F32)


def qkv_kernel(*refs):
    blocks = refs[:8]
    wq, wk, wv, frames, kv_own, kv_c, q_own, q_c = refs[8:]
    first = lax.axis_index("c") == 0
    x, yl = lax.axis_index("x"), lax.axis_index("yl")

    def project(w):
        total = None
        for j, (dx, dy) in enumerate(SHIFTS):
            source = ((x + 4 - dx) % 4) * 2 + (yl + dy) % 2
            rows = pl.ds(pl.multiple_of(source * BLK, BLK), BLK)
            term = jnp.dot(blocks[j][...], w[rows, :], preferred_element_type=F32)
            total = term if total is None else total + term
        left, right = total[:, :HEAD], total[:, HEAD:]
        mine = jnp.where(first, left, right).astype(BF16)
        other = jnp.where(first, right, left).astype(BF16)
        return mine, other

    tail = jnp.broadcast_to(frames[...], (16, BLK)).astype(BF16)
    kv_own[:BLK, :HEAD], kv_c[:BLK, :HEAD] = project(wk)
    kv_own[:BLK, HEAD:], kv_c[:BLK, HEAD:] = project(wv)
    kv_own[BLK:, :] = tail
    kv_c[BLK:, :] = tail
    q_own[:BLK, :], q_c[:BLK, :] = project(wq)
    for q in (q_own, q_c):
        q[BLK : BLK + 16, :] = tail[:, :HEAD]
        q[BLK + 16 :, :] = tail[:, HEAD:]


def qkv(blocks, wq, wk, wv, frames):
    kv = jax.ShapeDtypeStruct((BLK + 16, 2 * HEAD), BF16)
    q = jax.ShapeDtypeStruct((BLK + 32, HEAD), BF16)
    return pl.pallas_call(
        qkv_kernel,
        out_shape=(kv, kv, q, q),
        in_specs=[VMEM] * 12,
        out_specs=(VMEM,) * 4,
        cost_estimate=pl.CostEstimate(
            flops=2 * BLK * 2048 * 768, bytes_accessed=5 << 20, transcendentals=0
        ),
        name="qkv",
    )(*blocks, wq, wk, wv, frames)


def visit(q_s, f_s, m_s, l_s, acc_s, pair, masked):
    scale = 1.0 / math.sqrt(HEAD)

    def columns():
        lines = [jnp.broadcast_to(kv[BLK : BLK + 1, :].astype(F32), (HEAD, BLK)) for kv in pair]
        return [jnp.transpose(line)[:, :1] for line in lines]

    key_frames = columns() if masked else None

    def part(i, carry):
        lanes = pl.ds(pl.multiple_of(i * BLK, BLK), BLK)
        old = m_s[:, lanes]
        top, scores, allowed = old, [], []
        for j, kv in enumerate(pair):
            s = nt_dot(kv[:BLK, :HEAD], q_s[lanes, :]) * scale
            if masked:
                ok = key_frames[j] <= f_s[:, lanes]
                s = jnp.where(ok, s, NEG)
                allowed.append(ok)
            scores.append(s)
            top = jnp.maximum(top, jnp.max(s, axis=0, keepdims=True))
        decay = jnp.exp(old - top)
        total, acc = l_s[:, lanes] * decay, acc_s[:, lanes] * decay
        for j, kv in enumerate(pair):
            p = jnp.exp(scores[j] - top)
            if masked:
                p = jnp.where(allowed[j], p, 0.0)
            total = total + jnp.sum(p, axis=0, keepdims=True)
            acc = acc + tn_dot(kv[:BLK, HEAD:], p.astype(BF16))
        m_s[:, lanes], l_s[:, lanes], acc_s[:, lanes] = top, total, acc
        return carry

    lax.fori_loop(0, 4, part, 0)


def local_kernel(q0, q1, q2, q3, kv_a, kv_b, q_s, f_s, m_s, l_s, acc_s):
    for g, q in enumerate((q0, q1, q2, q3)):
        q_s[g * BLK : (g + 1) * BLK, :] = q[:BLK, :]
        for half in range(2):
            lanes = slice(g * BLK + half * HEAD, g * BLK + (half + 1) * HEAD)
            f_s[:, lanes] = q[BLK + 16 * half : BLK + 16 * half + 1, :].astype(F32)
    m_s[...] = jnp.full_like(m_s, NEG)
    l_s[...] = jnp.zeros_like(l_s)
    acc_s[...] = jnp.zeros_like(acc_s)
    visit(q_s, f_s, m_s, l_s, acc_s, (kv_a, kv_b), True)


STATE = (
    jax.ShapeDtypeStruct((4 * BLK, HEAD), BF16),
    jax.ShapeDtypeStruct((1, 4 * BLK), F32),
    jax.ShapeDtypeStruct((1, 4 * BLK), F32),
    jax.ShapeDtypeStruct((1, 4 * BLK), F32),
    jax.ShapeDtypeStruct((HEAD, 4 * BLK), F32),
)


def visit_cost(blocks):
    work = 1024 * BLK * blocks
    return pl.CostEstimate(flops=4 * work * HEAD, bytes_accessed=2 << 20, transcendentals=work)


def local(q0, q1, q2, q3, kv_a, kv_b):
    return pl.pallas_call(
        local_kernel,
        out_shape=STATE,
        in_specs=[VMEM] * 6,
        out_specs=(VMEM,) * 5,
        cost_estimate=visit_cost(4),
        name="local",
    )(q0, q1, q2, q3, kv_a, kv_b)


def step_kernel(k, q_s, f_s, m_i, l_i, acc_i, fa, fb, ba, bb, m_s, l_s, acc_s):
    z = lax.axis_index("z")
    m_s[...] = m_i[...]
    l_s[...] = l_i[...]
    acc_s[...] = acc_i[...]

    @pl.when(z >= k)
    def _():
        visit(q_s, f_s, m_s, l_s, acc_s, (fa, fb), False)

    @pl.when(z + k >= 8)
    def _():
        visit(q_s, f_s, m_s, l_s, acc_s, (ba, bb), False)

    if k == 1:

        @pl.when((z < 7) & (lax.axis_index("yh") == 0))
        def _():
            visit(q_s, f_s, m_s, l_s, acc_s, (ba, bb), True)


def step(k, state, fa, fb, ba, bb):
    m, l, acc = pl.pallas_call(
        functools.partial(step_kernel, k),
        out_shape=STATE[2:],
        in_specs=[VMEM] * 9,
        out_specs=(VMEM,) * 3,
        cost_estimate=visit_cost(4),
        name="step",
    )(*state, fa, fb, ba, bb)
    return state[0], state[1], m, l, acc


def last_kernel(q_s, f_s, m_i, l_i, acc_i, a, b, o0, o1, o2, o3, m_s, l_s, acc_s):
    m_s[...] = m_i[...]
    l_s[...] = l_i[...]
    acc_s[...] = acc_i[...]

    @pl.when(lax.axis_index("z") >= 4)
    def _():
        visit(q_s, f_s, m_s, l_s, acc_s, (a, b), False)

    for g, out in enumerate((o0, o1, o2, o3)):
        lanes = slice(g * BLK, (g + 1) * BLK)
        total = l_s[:, lanes]
        some = total > 0.0
        safe = jnp.where(some, total, 1.0)
        out[:HEAD, :] = acc_s[:, lanes] / safe
        lse = jnp.where(some, m_s[:, lanes] + jnp.log(safe), NEG)
        out[HEAD:, :] = jnp.broadcast_to(lse, (8, BLK))


def last(state, a, b):
    return pl.pallas_call(
        last_kernel,
        out_shape=(jax.ShapeDtypeStruct((HEAD + 8, BLK), F32),) * 4,
        in_specs=[VMEM] * 7,
        out_specs=(VMEM,) * 4,
        scratch_shapes=[pltpu.VMEM(s.shape, s.dtype) for s in STATE[2:]],
        cost_estimate=visit_cost(2),
        name="last",
    )(*state, a, b)


def merge_kernel(a0, a1, b0, b1, w, out):
    c = lax.axis_index("c")

    def merged(a, b):
        la, lb = a[HEAD : HEAD + 1, :], b[HEAD : HEAD + 1, :]
        top = jnp.maximum(la, lb)
        wa, wb = jnp.exp(la - top), jnp.exp(lb - top)
        inv = 1.0 / (wa + wb)
        return (a[:HEAD, :] * (wa * inv) + b[:HEAD, :] * (wb * inv)).astype(BF16)

    mine, other = merged(a0, a1), merged(b0, b1)
    rows_mine = pl.ds(pl.multiple_of(c * HEAD, HEAD), HEAD)
    rows_other = pl.ds(pl.multiple_of((1 - c) * HEAD, HEAD), HEAD)
    for t in range(8):
        cols = slice(t * BLK, (t + 1) * BLK)
        out[t] = (tn_dot(mine, w[rows_mine, cols]) + tn_dot(other, w[rows_other, cols])).astype(BF16)


def merge(a0, a1, b0, b1, w):
    return pl.pallas_call(
        merge_kernel,
        out_shape=jax.ShapeDtypeStruct((8, BLK, BLK), BF16),
        in_specs=[VMEM] * 5,
        out_specs=VMEM,
        cost_estimate=pl.CostEstimate(
            flops=2 * BLK * BLK * 2048, bytes_accessed=3 << 20, transcendentals=1024
        ),
        name="merge",
    )(a0, a1, b0, b1, w)


def slots_kernel(parts, stream, slot, mixed, rows):
    total = stream[...].astype(F32) + jnp.sum(parts[...].astype(F32), axis=0)
    kept = total.astype(BF16)
    mixed[...] = kept
    ids = lax.broadcasted_iota(jnp.int32, (EXPERTS * CAP, BLK), 0)
    pick = jnp.where(ids == slot[...], 1.0, 0.0).astype(BF16)
    rows[...] = jnp.dot(pick, kept, preferred_element_type=F32).astype(BF16)


def to_slots(parts, stream, slot):
    return pl.pallas_call(
        slots_kernel,
        out_shape=(
            jax.ShapeDtypeStruct((BLK, BLK), BF16),
            jax.ShapeDtypeStruct((EXPERTS * CAP, BLK), BF16),
        ),
        in_specs=[VMEM] * 3,
        out_specs=(VMEM, VMEM),
        cost_estimate=pl.CostEstimate(
            flops=2 * 512 * BLK * BLK, bytes_accessed=2 << 20, transcendentals=0
        ),
        name="slots",
    )(parts, stream, slot)


GATES = 768


def expert_kernel(x, gain, g0, g1, u0, u1, d0, d1, out, n_s, w1, w2, sem):
    units = g0.shape[0]

    def copies(some):
        places = [(g0, w1, 0), (g1, w1, units), (u0, w1, GATES), (u1, w1, GATES + units), (d0, w2, 0), (d1, w2, units)]
        return [
            pltpu.make_async_copy(src, dst.at[pl.ds(at, units), :], sem.at[i])
            for i, (src, dst, at) in list(enumerate(places))[some]
        ]

    first = pl.program_id(0) == 0

    @pl.when(first)
    def _():
        for copy in copies(slice(0, 6)):
            copy.start()
        pad = jnp.zeros((GATES - 2 * units, 2048), BF16)
        w1[2 * units : GATES, :] = pad
        w1[GATES + 2 * units :, :] = pad
        w2[2 * units :, :] = pad

    square = None
    for t in range(8):
        v = x[t].astype(F32)
        term = jnp.sum(v * v, axis=1, keepdims=True)
        square = term if square is None else square + term
    inv = lax.rsqrt(square * (1.0 / 2048) + NORM_EPS)
    for t in range(8):
        cols = slice(t * BLK, (t + 1) * BLK)
        n_s[:, cols] = (x[t].astype(F32) * inv * gain[:, cols]).astype(BF16)

    @pl.when(first)
    def _():
        for copy in copies(slice(0, 4)):
            copy.wait()

    both = nt_dot(n_s[...], w1[...])
    g, u = both[:, :GATES], both[:, GATES:]
    hidden = (g / (1.0 + jnp.exp(-g)) * u).astype(BF16)

    @pl.when(first)
    def _():
        for copy in copies(slice(4, 6)):
            copy.wait()

    for t in range(8):
        cols = slice(t * BLK, (t + 1) * BLK)
        out[t] = jnp.dot(hidden, w2[:, cols], preferred_element_type=F32).astype(BF16)


def expert(x, gain, gates, ups, downs):
    rows = 128
    units = gates[0].shape[0]
    hbm = pl.BlockSpec(memory_space=pl.ANY)
    return pl.pallas_call(
        expert_kernel,
        out_shape=jax.ShapeDtypeStruct(x.shape, BF16),
        grid=(x.shape[1] // rows,),
        in_specs=[
            pl.BlockSpec((8, rows, BLK), lambda j: (0, j, 0)),
            pl.BlockSpec((1, 2048), lambda j: (0, 0)),
        ]
        + [hbm] * 6,
        out_specs=pl.BlockSpec((8, rows, BLK), lambda j: (0, j, 0)),
        scratch_shapes=[
            pltpu.VMEM((rows, 2048), BF16),
            pltpu.VMEM((2 * GATES, 2048), BF16),
            pltpu.VMEM((GATES, 2048), BF16),
            pltpu.SemaphoreType.DMA((6,)),
        ],
        cost_estimate=pl.CostEstimate(
            flops=12 * 512 * 2048 * units, bytes_accessed=13 << 20, transcendentals=1024 * units
        ),
        name="expert",
    )(x, gain, *gates, *ups, *downs)


def finish_kernel(mixed, rows, slot, out):
    ids = lax.broadcasted_iota(jnp.int32, (EXPERTS * CAP, BLK), 0)
    pick = jnp.where(ids == slot[...], 1.0, 0.0).astype(BF16)
    out[...] = (mixed[...].astype(F32) + tn_dot(pick, rows[...])).astype(BF16)


def finish(mixed, rows, slot):
    return pl.pallas_call(
        finish_kernel,
        out_shape=jax.ShapeDtypeStruct((BLK, BLK), BF16),
        in_specs=[VMEM] * 3,
        out_specs=VMEM,
        cost_estimate=pl.CostEstimate(
            flops=2 * 512 * BLK * BLK, bytes_accessed=1 << 20, transcendentals=0
        ),
        name="finish",
    )(mixed, rows, slot)


def tp_shift(a, dx, dy):
    pairs = [(i * 2 + j, ((i + dx) % 4) * 2 + (j + dy) % 2) for i in range(4) for j in range(2)]
    return lax.ppermute(a, TP, pairs)


def swap(a, dy, dc):
    pairs = [(i * 2 + j, (i ^ dy) * 2 + (j ^ dc)) for i in range(2) for j in range(2)]
    return lax.ppermute(a, ("yh", "c"), pairs)


def ring(a, step):
    return lax.ppermute(a, "z", [(i, (i + step) % 8) for i in range(8)])


def attention(q_own, q_c, kv_own, kv_c):
    kv_b = swap(kv_c, 0, 1)
    fa, ba = ring(kv_own, 1), ring(kv_own, -1)
    qs = (q_own, swap(q_c, 0, 1), swap(q_own, 1, 0), swap(q_c, 1, 1))
    fb, bb = ring(kv_b, 1), ring(kv_b, -1)
    state = local(*qs, kv_own, kv_b)
    for k in range(1, 4):
        here = (fa, fb, ba, bb)
        if k > 1:
            held = lax.optimization_barrier((*here, *state))
            here, state = held[:4], held[4:]
        fa, fb, ba, bb = here
        if k < 3:
            fa, ba, fb, bb = ring(fa, 1), ring(ba, -1), ring(fb, 1), ring(bb, -1)
        else:
            fa, bb = ring(fa, 1), ring(bb, -1)
        state = step(k, state, *here)
    return last(state, fa, bb)


def shards(stream, frames, fidelity, wq, wk, wv, wo, gain, gate, up, down):
    blocks = [stream if s == (0, 0) else tp_shift(stream, *s) for s in SHIFTS]

    route = fidelity[:, 0]
    spot = lax.iota(jnp.int32, BLK)
    same = (route[:, None] == route[None, :]) & (spot[None, :] < spot[:, None])
    slot = (route * CAP + jnp.sum(same.astype(jnp.int32), axis=1))[None, :]

    kv_own, kv_c, q_own, q_c = qkv(blocks, wq, wk, wv, frames[None, :])
    own = (gate[0].T, up[0].T, down[0])
    *sending, q_c = lax.optimization_barrier((*own, q_c))
    far = [lax.ppermute(w, "c", [(0, 1), (1, 0)]) for w in sending]

    p0, p1, p2, p3 = attention(q_own, q_c, kv_own, kv_c)
    b0, a1, b1 = swap(p1, 0, 1), swap(p2, 1, 0), swap(p3, 1, 1)
    projected = merge(p0, a1, b0, b1, wo)
    parts = lax.all_to_all(projected, TP, 0, 0, tiled=True)
    mixed, rows = to_slots(parts, stream, slot)

    sent = lax.all_to_all(rows.reshape(EXPERTS, CAP, BLK), CHIPS, 0, 0, tiled=True)
    sent = jnp.broadcast_to(sent.reshape(1, EXPERTS * CAP, BLK), (8, EXPERTS * CAP, BLK))
    full = lax.all_to_all(sent, TP, 0, 0, tiled=True)
    lowered = expert(full, gain[None, :], *zip(own, far))
    pieces = lax.all_to_all(lowered, TP, 0, 0, tiled=True)
    summed = jnp.sum(pieces.astype(F32), axis=0).astype(BF16)
    back = lax.all_to_all(summed.reshape(EXPERTS, CAP, BLK), CHIPS, 0, 0, tiled=True)
    return finish(mixed, back.reshape(EXPERTS * CAP, BLK), slot)


def solution(mesh):
    axes = ("z", "yh", "c", "x", "yl")
    fine = Mesh(np.asarray(mesh.devices).reshape(8, 2, 2, 4, 2), axes)
    return jax.shard_map(
        shards,
        mesh=fine,
        in_specs=(
            P(SEQ, TP),
            P(SEQ),
            P(SEQ, None),
            P(None, TP),
            P(None, TP),
            P(None, TP),
            P(TP, None),
            P(),
            P(SEQ, None, TP),
            P(SEQ, None, TP),
            P(SEQ, TP, None),
        ),
        out_specs=P(SEQ, TP),
        check_vma=False,
    )
```

time: 266 us -> 241 us (0.906)
  waiting for transfers between devices: 98.9 us -> 61.8 us
  starting transfers between devices: 30.6 us -> 55.2 us
  Pallas kernels: 30.4 us -> 44 us
  between operations: 13.5 us -> 0.28 us
  blocking collectives: 76.5 us -> 69.7 us
  other arithmetic: 5.9 us -> 1.15 us
    all_gather x2 -> x0, waiting for transfers between devices: 67.1 us -> none  [the longest x1 34.4 us: shards(): full = lax.all_gather(sent.reshape(EXPERTS * CAP, BLK), ('c',) + TP, axis=0)]
    ppermute x2 -> x17, starting transfers between devices: 7.14 us -> 24.9 us  [the longest x14 24.3 us: ring(): return lax.ppermute(a, 'z', [(i, (i + step) % 8) for i in range(8)])]
    all_to_all x0 -> x1, waiting for transfers between devices: none -> 16.5 us  [shards(): full = lax.all_to_all(sent, TP, 0, 0, tiled=True)]
    ppermute x2 -> x17, waiting for transfers between devices: 4.95 us -> 14.9 us  [the longest x14 8.32 us: ring(): return lax.ppermute(a, 'z', [(i, (i + step) % 8) for i in range(8)])]
    pallas_call x2 -> x6, Pallas kernels: 10.4 us -> 19.7 us  [the longest x3 9.07 us: step(): pl.pallas_call(functools.partial(step_kernel, k), out_shape=STATE[2:], in...]
    all_to_all x0 -> x1, starting transfers between devices: none -> 7.16 us  [shards(): full = lax.all_to_all(sent, TP, 0, 0, tiled=True)]
    ppermute x7, waiting for transfers between devices: 3.19 us -> 9.06 us  [tp_shift(): return lax.ppermute(a, TP, pairs)]
    squeeze x2 -> x0, local copies, waits for them, and re-layouts: 4.88 us -> none  [the longest x1 3.08 us: shards(): given = lax.dynamic_index_in_dim(lowered, 1 - c, 0, keepdims=False)]
  transfers between devices with their start and end apart: 18 -> 33, of which waited for: 12 -> 15; matrix products, arithmetic and copies ran while one was open for 1% -> 0% of each run, Pallas kernels for 0% -> 6%
where the time goes in v2:
time: 241 us; the launch traced here: 240 us
  blocking collectives  69.7 us (29%)
  waiting for transfers between devices  61.8 us (26%)
  starting transfers between devices  55.2 us (23%)
  Pallas kernels  44 us (18%)
  local copies, waits for them, and re-layouts  7.66 us (3%)
    all_to_all x1, blocking collectives, shards(): pieces = lax.all_to_all(lowered, TP, 0, 0, tiled=True)  30.7 us
    ppermute x14, starting transfers between devices, ring(): return lax.ppermute(a, 'z', [(i, (i + step) % 8) for i in range(8)])  24.3 us
    all_to_all x1, blocking collectives, shards(): lax.all_to_all(rows.reshape(EXPERTS, CAP, BLK), CHIPS, 0, 0, tiled=True)  22 us
    all_to_all x1, blocking collectives, shards(): lax.all_to_all(summed.reshape(EXPERTS, CAP, BLK), CHIPS, 0, 0, tiled=True)  17 us
    pallas_call x1, Pallas kernels, expert(): pl.pallas_call(expert_kernel, out_shape=jax.ShapeDtypeStruct(x.shape, BF1...  16.7 us
    all_to_all x1, waiting for transfers between devices, shards(): full = lax.all_to_all(sent, TP, 0, 0, tiled=True)  16.5 us
    all_to_all x1, waiting for transfers between devices, shards(): parts = lax.all_to_all(projected, TP, 0, 0, tiled=True)  13.9 us
    ppermute x7, starting transfers between devices, tp_shift(): return lax.ppermute(a, TP, pairs)  10.2 us
  transfers between devices with their start and end apart: 33, of which 15 were waited for; matrix products, arithmetic and copies ran while one was open for 0% of the time, Pallas kernels for 6%

profile of v2, /device:TPU:6, one launch (start us, length us, event | category | flops | bytes accessed | tf_op | source)
XLA Modules:
  0.0 239.8 jit_solution(7174843783253766195)
XLA Ops:
  11.3 4.1 %collective-permute-done.4.refs_5_ = bf16[256,256]{1,0:T(8,128)(2,1)S(1)} collective-permute-done((bf16[256,256]{1,0:T(8,128)(2,1)}, bf16[256,256]{1,0:T(8,128)(2,1)S(1)}, u32[]{:S(2)}, u32[]{:S(2)}) %collective-permute-start.4) | collective-permute-done | bytes 131104 | tf_op jit(solution)/shard_map/ppermute | solution.py:374
  20.0 4.1 %qkv.1 = (bf16[272,256]{1,0:T(8,128)(2,1)}, bf16[272,256]{1,0:T(8,128)(2,1)}, bf16[288,128]{1,0:T(8,128)(2,1)}, bf16[288,128]{1,0:T(8,128)(2,1)}) custom-call(bf16[256,256]{1,0:T(8,128)(2,1)} %stream.1, bf16[256,256]{1,0:T(8,128)(2,1)} %copy-done.7, bf16[256,256]{1,0:T(8,128)(2,1)} %copy-done.8, bf16[256,256]{1,0:T(8,128)(2,1)} %copy-done.9, ...), custom_call_target="tpu_custom_call" | custom-call | flops 805306368 | bytes 5242880 | tf_op jit(solution)/shard_map/qkv/pallas_call | solution.py:69
  26.4 3.9 %collective-permute-start.12 = (bf16[272,256]{1,0:T(8,128)(2,1)}, bf16[272,256]{1,0:T(8,128)(2,1)S(1)}, u32[]{:S(2)}, u32[]{:S(2)}) collective-permute-start(bf16[272,256]{1,0:T(8,128)(2,1)} %get-tuple-element.51.kv_a), channel_id=1, source_target_pairs={{0,224},{32,0},{64,32},{96,64},{128,96},{160,128},{192,160},{224,1... | collective-permute-start | bytes 417800 | tf_op jit(solution)/shard_map/ppermute | solution.py:383
  30.4 3.2 %collective-permute-start.14 = (bf16[272,256]{1,0:T(8,128)(2,1)S(1)}, bf16[272,256]{1,0:T(8,128)(2,1)S(1)}, u32[]{:S(2)}, u32[]{:S(2)}) collective-permute-start(bf16[272,256]{1,0:T(8,128)(2,1)S(1)} %collective-permute-done.9.kv_b), channel_id=1, source_target_pairs={{0,224},{32,0},{64,32},{96,64},{128,96},{160,128},{192,160},{224,1... | collective-permute-start | bytes 417800 | tf_op jit(solution)/shard_map/ppermute | solution.py:383
  33.6 3.1 %collective-permute-start.17 = (bf16[288,128]{1,0:T(8,128)(2,1)}, bf16[288,128]{1,0:T(8,128)(2,1)S(1)}, u32[]{:S(2)}, u32[]{:S(2)}) collective-permute-start(bf16[288,128]{1,0:T(8,128)(2,1)} %get-tuple-element.53.q0), channel_id=1, source_target_pairs={{0,16},{8,24},{16,0},{24,8},{1,17},{9,25},{17,1},{25,9},{2,18},{10... | collective-permute-start | bytes 221192 | tf_op jit(solution)/shard_map/ppermute | solution.py:379
  36.8 2.9 %collective-permute-done.17.q2 = bf16[288,128]{1,0:T(8,128)(2,1)S(1)} collective-permute-done((bf16[288,128]{1,0:T(8,128)(2,1)}, bf16[288,128]{1,0:T(8,128)(2,1)S(1)}, u32[]{:S(2)}, u32[]{:S(2)}) %collective-permute-start.17) | collective-permute-done | bytes 73760 | tf_op jit(solution)/shard_map/ppermute | solution.py:379
  40.6 3.2 %collective-permute-start.13 = (bf16[272,256]{1,0:T(8,128)(2,1)S(1)}, bf16[272,256]{1,0:T(8,128)(2,1)S(1)}, u32[]{:S(2)}, u32[]{:S(2)}) collective-permute-start(bf16[272,256]{1,0:T(8,128)(2,1)S(1)} %collective-permute-done.12.ba), channel_id=1, source_target_pairs={{0,224},{32,0},{64,32},{96,64},{128,96},{160,128},{192,160},{224,1... | collective-permute-start | bytes 417800 | tf_op jit(solution)/shard_map/ppermute | solution.py:383
  43.8 3.2 %collective-permute-start.15 = (bf16[272,256]{1,0:T(8,128)(2,1)S(1)}, bf16[272,256]{1,0:T(8,128)(2,1)S(1)}, u32[]{:S(2)}, u32[]{:S(2)}) collective-permute-start(bf16[272,256]{1,0:T(8,128)(2,1)S(1)} %collective-permute-done.14.bb), channel_id=1, source_target_pairs={{0,224},{32,0},{64,32},{96,64},{128,96},{160,128},{192,160},{224,1... | collective-permute-start | bytes 417800 | tf_op jit(solution)/shard_map/ppermute | solution.py:383
  47.7 4.4 %local.1 = (bf16[1024,128]{1,0:T(8,128)(2,1)}, f32[1,1024]{1,0:T(1,128)}, f32[1,1024]{1,0:T(1,128)}, f32[1,1024]{1,0:T(1,128)}, f32[128,1024]{1,0:T(8,128)}) custom-call(bf16[288,128]{1,0:T(8,128)(2,1)} %get-tuple-element.53.q0, bf16[288,128]{1,0:T(8,128)(2,1)} %copy-done.31, bf16[288,128]{1,0:T(8,128)(2,1)} %copy-done.32, bf16[288,128]{1,0:T(8,128)(2,1)} %copy-done.33, ...), custom_call_target="tpu_custom_call" | custom-call | flops 536870912 | bytes 2097152 | tf_op jit(solution)/shard_map/local/pallas_call | solution.py:143
  52.2 4.7 %step.3 = (f32[1,1024]{1,0:T(1,128)}, f32[1,1024]{1,0:T(1,128)}, f32[128,1024]{1,0:T(8,128)}) custom-call(bf16[1024,128]{1,0:T(8,128)(2,1)} %get-tuple-element.76.q_s, f32[1,1024]{1,0:T(1,128)} %get-tuple-element.77.f_s, f32[1,1024]{1,0:T(1,128)} %get-tuple-element.58.m_i, f32[1,1024]{1,0:T(1,128)} %get-tuple-element.59.l_i, ...), custom_call_target="tpu_custom_call" | custom-call | flops 536870912 | bytes 2097152 | tf_op jit(solution)/shard_map/step/pallas_call | solution.py:175
  64.5 2.9 %collective-permute-done.20.fb = bf16[272,256]{1,0:T(8,128)(2,1)S(1)} collective-permute-done((bf16[272,256]{1,0:T(8,128)(2,1)S(1)}, bf16[272,256]{1,0:T(8,128)(2,1)S(1)}, u32[]{:S(2)}, u32[]{:S(2)}) %collective-permute-start.20) | collective-permute-done | bytes 139296 | tf_op jit(solution)/shard_map/ppermute | solution.py:383
  69.0 3.4 %collective-permute-start.23 = (bf16[272,256]{1,0:T(8,128)(2,1)S(1)}, bf16[272,256]{1,0:T(8,128)(2,1)S(1)}, u32[]{:S(2)}, u32[]{:S(2)}) collective-permute-start(bf16[272,256]{1,0:T(8,128)(2,1)S(1)} %collective-permute-done.19.fa), channel_id=1, source_target_pairs={{0,32},{32,64},{64,96},{96,128},{128,160},{160,192},{192,224},{224... | collective-permute-start | bytes 417800 | tf_op jit(solution)/shard_map/ppermute | solution.py:383
  81.2 3.6 %collective-permute-start.27 = (f32[136,256]{1,0:T(8,128)}, f32[136,256]{1,0:T(8,128)S(1)}, u32[]{:S(2)}, u32[]{:S(2)}) collective-permute-start(f32[136,256]{1,0:T(8,128)} %get-tuple-element.91), channel_id=1, source_target_pairs={{0,24},{8,16},{16,8},{24,0},{1,25},{9,17},{17,9},{25,1},{2,26},{10... | collective-permute-start | bytes 417800 | tf_op jit(solution)/shard_map/ppermute | solution.py:379
  84.8 4.4 %collective-permute-done.25.a1 = f32[136,256]{1,0:T(8,128)S(1)} collective-permute-done((f32[136,256]{1,0:T(8,128)}, f32[136,256]{1,0:T(8,128)S(1)}, u32[]{:S(2)}, u32[]{:S(2)}) %collective-permute-start.25) | collective-permute-done | bytes 139296 | tf_op jit(solution)/shard_map/ppermute | solution.py:379
  90.0 3.3 %merge.1 = bf16[8,256,256]{2,1,0:T(8,128)(2,1)} custom-call(f32[136,256]{1,0:T(8,128)} %get-tuple-element.88.a0, f32[136,256]{1,0:T(8,128)} %copy-done.4, f32[136,256]{1,0:T(8,128)} %copy-done.5, f32[136,256]{1,0:T(8,128)} %copy-done.6, bf16[256,2048]{1,0:T(8,128)(2,1)} %w.1), custom_call_target="tpu_custom_call" | custom-call | flops 268435456 | bytes 3145728 | tf_op jit(solution)/shard_map/merge/pallas_call | solution.py:236
  93.3 4.8 %all-to-all-start = ((bf16[8,256,256]{2,1,0:T(8,128)(2,1)}), bf16[8,256,256]{2,1,0:T(8,128)(2,1)S(1)}, u32[]{:S(2)}, u32[]{:S(2)}) async-start(bf16[8,256,256]{2,1,0:T(8,128)(2,1)} %merge.1), calls=%async_computation | async-start | bytes 2097152 | tf_op jit(solution)/shard_map/all_to_all | solution.py:422
  98.9 13.9 %all-to-all-done.parts = bf16[8,256,256]{2,1,0:T(8,128)(2,1)S(1)} async-done(((bf16[8,256,256]{2,1,0:T(8,128)(2,1)}), bf16[8,256,256]{2,1,0:T(8,128)(2,1)S(1)}, u32[]{:S(2)}, u32[]{:S(2)}) %all-to-all-start) | async-done | bytes 1048608 | tf_op jit(solution)/shard_map/all_to_all | solution.py:422
  116.3 22.0 %all_to_all.25 = bf16[16,32,256]{2,1,0:T(8,128)(2,1)S(1)} all-to-all(bf16[16,32,256]{2,1,0:T(8,128)(2,1)} %bitcast.20), channel_id=1, replica_groups=mesh['z'=8,'yh'=2,'c'=2,'x'=4,'yl'=2] {'z','yh'}, dimensions={0} | all-to-all | bytes 524288 | tf_op jit(solution)/shard_map/all_to_all | solution.py:425
  139.8 7.2 %all-to-all-start.2 = ((bf16[8,512,256]{2,1,0:T(8,128)(2,1)}), bf16[8,512,256]{2,1,0:T(8,128)(2,1)S(1)}, u32[]{:S(2)}, u32[]{:S(2)}) async-start(bf16[8,512,256]{2,1,0:T(8,128)(2,1)} %broadcast_in_dim.18), calls=%async_computation.2 | async-start | bytes 4194304 | tf_op jit(solution)/shard_map/all_to_all | solution.py:427
  147.6 3.8 %collective-permute-done.28.g1 = bf16[352,2048]{1,0:T(8,128)(2,1)S(1)} collective-permute-done((bf16[352,2048]{1,0:T(8,128)(2,1)S(1)}, bf16[352,2048]{1,0:T(8,128)(2,1)S(1)}, u32[]{:S(2)}, u32[]{:S(2)}) %collective-permute-start.28) | collective-permute-done | bytes 1441824 | tf_op jit(solution)/shard_map/ppermute | solution.py:417
  155.2 16.5 %all-to-all-done.2.x = bf16[8,512,256]{2,1,0:T(8,128)(2,1)S(1)} async-done(((bf16[8,512,256]{2,1,0:T(8,128)(2,1)}), bf16[8,512,256]{2,1,0:T(8,128)(2,1)S(1)}, u32[]{:S(2)}, u32[]{:S(2)}) %all-to-all-start.2) | async-done | bytes 2097184 | tf_op jit(solution)/shard_map/all_to_all | solution.py:427
  173.1 16.7 %expert.1 = bf16[8,512,256]{2,1,0:T(8,128)(2,1)} custom-call(bf16[8,512,256]{2,1,0:T(8,128)(2,1)} %copy-done.1, f32[1,2048]{1,0:T(1,128)} %bitcast.30, bf16[352,2048]{1,0:T(8,128)(2,1)} %bitcast.24, bf16[352,2048]{1,0:T(8,128)(2,1)} %copy-done.16, bf16[352,2048]{1,0:T(8,128)(2,1)} %bitcast.27, bf16[352,2048]{1,0:T(8,128)(2,1)} %copy-done.17, ...), custom_call_target="tpu_custom_call" | custom-call | flops 4429185024 | bytes 13631488 | tf_op jit(solution)/shard_map/expert/pallas_call | solution.py:330
  189.8 30.7 %all_to_all.26 = bf16[8,512,256]{2,1,0:T(8,128)(2,1)S(1)} all-to-all(bf16[8,512,256]{2,1,0:T(8,128)(2,1)} %expert.1), channel_id=1, replica_groups=mesh['z'=8,'yh'=2,'c'=2,'x'=4,'yl'=2] {'x','yl'}, dimensions={0} | all-to-all | bytes 4194304 | tf_op jit(solution)/shard_map/all_to_all | solution.py:429
  220.9 17.0 %all_to_all.27 = bf16[16,32,256]{2,1,0:T(8,128)(2,1)} all-to-all(bf16[16,32,256]{2,1,0:T(8,128)(2,1)S(1)} %bitcast.17), channel_id=1, replica_groups=mesh['z'=8,'yh'=2,'c'=2,'x'=4,'yl'=2] {'z','yh'}, dimensions={0} | all-to-all | bytes 524288 | tf_op jit(solution)/shard_map/all_to_all | solution.py:431
  (127 shorter events, 52.4 us)
Async XLA Ops:
  0.0 8.0 %collective-permute-start = (bf16[256,256]{1,0:T(8,128)(2,1)}, bf16[256,256]{1,0:T(8,128)(2,1)S(1)}, u32[]{:S(2)}, u32[]{:S(2)}) collective-permute-start(bf16[256,256]{1,0:T(8,128)(2,1)} %stream.1), channel_id=1, source_target_pairs={{0,1},{1,0},{2,3},{3,2},{4,5},{5,4},{6,7},{7,6},{8,9},{9,8},{10,11... | collective-permute-start | bytes 393224 | tf_op jit(solution)/shard_map/ppermute | solution.py:374
  2.2 8.8 %collective-permute-start.2 = (bf16[256,256]{1,0:T(8,128)(2,1)}, bf16[256,256]{1,0:T(8,128)(2,1)S(1)}, u32[]{:S(2)}, u32[]{:S(2)}) collective-permute-start(bf16[256,256]{1,0:T(8,128)(2,1)} %stream.1), channel_id=1, source_target_pairs={{0,3},{1,2},{2,5},{3,4},{4,7},{5,6},{6,1},{7,0},{8,11},{9,10},{10,... | collective-permute-start | bytes 393224 | tf_op jit(solution)/shard_map/ppermute | solution.py:374
  3.7 7.6 %collective-permute-start.3 = (bf16[256,256]{1,0:T(8,128)(2,1)}, bf16[256,256]{1,0:T(8,128)(2,1)S(1)}, u32[]{:S(2)}, u32[]{:S(2)}) collective-permute-start(bf16[256,256]{1,0:T(8,128)(2,1)} %stream.1), channel_id=1, source_target_pairs={{0,4},{1,5},{2,6},{3,7},{4,0},{5,1},{6,2},{7,3},{8,12},{9,13},{10,... | collective-permute-start | bytes 393224 | tf_op jit(solution)/shard_map/ppermute | solution.py:374
  5.6 9.8 %collective-permute-start.4 = (bf16[256,256]{1,0:T(8,128)(2,1)}, bf16[256,256]{1,0:T(8,128)(2,1)S(1)}, u32[]{:S(2)}, u32[]{:S(2)}) collective-permute-start(bf16[256,256]{1,0:T(8,128)(2,1)} %stream.1), channel_id=1, source_target_pairs={{0,5},{1,4},{2,7},{3,6},{4,1},{5,0},{6,3},{7,2},{8,13},{9,12},{10,... | collective-permute-start | bytes 393224 | tf_op jit(solution)/shard_map/ppermute | solution.py:374
  8.0 8.7 %collective-permute-start.5 = (bf16[256,256]{1,0:T(8,128)(2,1)}, bf16[256,256]{1,0:T(8,128)(2,1)S(1)}, u32[]{:S(2)}, u32[]{:S(2)}) collective-permute-start(bf16[256,256]{1,0:T(8,128)(2,1)} %stream.1), channel_id=1, source_target_pairs={{0,6},{1,7},{2,0},{3,1},{4,2},{5,3},{6,4},{7,5},{8,14},{9,15},{10,... | collective-permute-start | bytes 393224 | tf_op jit(solution)/shard_map/ppermute | solution.py:374
  8.7 10.6 %collective-permute-start.6 = (bf16[256,256]{1,0:T(8,128)(2,1)}, bf16[256,256]{1,0:T(8,128)(2,1)S(1)}, u32[]{:S(2)}, u32[]{:S(2)}) collective-permute-start(bf16[256,256]{1,0:T(8,128)(2,1)} %stream.1), channel_id=1, source_target_pairs={{0,7},{1,6},{2,1},{3,0},{4,3},{5,2},{6,5},{7,4},{8,15},{9,14},{10,... | collective-permute-start | bytes 393224 | tf_op jit(solution)/shard_map/ppermute | solution.py:374
  24.0 9.6 %collective-permute-start.16 = (bf16[288,128]{1,0:T(8,128)(2,1)}, bf16[288,128]{1,0:T(8,128)(2,1)S(1)}, u32[]{:S(2)}, u32[]{:S(2)}) collective-permute-start(bf16[288,128]{1,0:T(8,128)(2,1)} %get-tuple-element.55), channel_id=1, source_target_pairs={{0,8},{8,0},{16,24},{24,16},{1,9},{9,1},{17,25},{25,17},{2,10},{10... | collective-permute-start | bytes 221192 | tf_op jit(solution)/shard_map/ppermute | solution.py:379
  24.5 16.0 %collective-permute-start.7 = (bf16[272,256]{1,0:T(8,128)(2,1)}, bf16[272,256]{1,0:T(8,128)(2,1)S(1)}, u32[]{:S(2)}, u32[]{:S(2)}) collective-permute-start(bf16[272,256]{1,0:T(8,128)(2,1)} %get-tuple-element.51.kv_a), channel_id=1, source_target_pairs={{0,32},{32,64},{64,96},{96,128},{128,160},{160,192},{192,224},{224... | collective-permute-start | bytes 417800 | tf_op jit(solution)/shard_map/ppermute | solution.py:383
  26.4 14.1 %collective-permute-start.12 = (bf16[272,256]{1,0:T(8,128)(2,1)}, bf16[272,256]{1,0:T(8,128)(2,1)S(1)}, u32[]{:S(2)}, u32[]{:S(2)}) collective-permute-start(bf16[272,256]{1,0:T(8,128)(2,1)} %get-tuple-element.51.kv_a), channel_id=1, source_target_pairs={{0,224},{32,0},{64,32},{96,64},{128,96},{160,128},{192,160},{224,1... | collective-permute-start | bytes 417800 | tf_op jit(solution)/shard_map/ppermute | solution.py:383
  30.4 13.4 %collective-permute-start.10 = (bf16[272,256]{1,0:T(8,128)(2,1)S(1)}, bf16[272,256]{1,0:T(8,128)(2,1)S(1)}, u32[]{:S(2)}, u32[]{:S(2)}) collective-permute-start(bf16[272,256]{1,0:T(8,128)(2,1)S(1)} %collective-permute-done.9.kv_b), channel_id=1, source_target_pairs={{0,32},{32,64},{64,96},{96,128},{128,160},{160,192},{192,224},{224... | collective-permute-start | bytes 417800 | tf_op jit(solution)/shard_map/ppermute | solution.py:383
  30.4 13.4 %collective-permute-start.14 = (bf16[272,256]{1,0:T(8,128)(2,1)S(1)}, bf16[272,256]{1,0:T(8,128)(2,1)S(1)}, u32[]{:S(2)}, u32[]{:S(2)}) collective-permute-start(bf16[272,256]{1,0:T(8,128)(2,1)S(1)} %collective-permute-done.9.kv_b), channel_id=1, source_target_pairs={{0,224},{32,0},{64,32},{96,64},{128,96},{160,128},{192,160},{224,1... | collective-permute-start | bytes 417800 | tf_op jit(solution)/shard_map/ppermute | solution.py:383
  40.6 16.3 %collective-permute-start.8 = (bf16[272,256]{1,0:T(8,128)(2,1)S(1)}, bf16[272,256]{1,0:T(8,128)(2,1)S(1)}, u32[]{:S(2)}, u32[]{:S(2)}) collective-permute-start(bf16[272,256]{1,0:T(8,128)(2,1)S(1)} %collective-permute-done.7.fa), channel_id=1, source_target_pairs={{0,32},{32,64},{64,96},{96,128},{128,160},{160,192},{192,224},{224... | collective-permute-start | bytes 417800 | tf_op jit(solution)/shard_map/ppermute | solution.py:383
  40.6 16.3 %collective-permute-start.13 = (bf16[272,256]{1,0:T(8,128)(2,1)S(1)}, bf16[272,256]{1,0:T(8,128)(2,1)S(1)}, u32[]{:S(2)}, u32[]{:S(2)}) collective-permute-start(bf16[272,256]{1,0:T(8,128)(2,1)S(1)} %collective-permute-done.12.ba), channel_id=1, source_target_pairs={{0,224},{32,0},{64,32},{96,64},{128,96},{160,128},{192,160},{224,1... | collective-permute-start | bytes 417800 | tf_op jit(solution)/shard_map/ppermute | solution.py:383
  43.8 13.1 %collective-permute-start.11 = (bf16[272,256]{1,0:T(8,128)(2,1)S(1)}, bf16[272,256]{1,0:T(8,128)(2,1)S(1)}, u32[]{:S(2)}, u32[]{:S(2)}) collective-permute-start(bf16[272,256]{1,0:T(8,128)(2,1)S(1)} %collective-permute-done.10.fb), channel_id=1, source_target_pairs={{0,32},{32,64},{64,96},{96,128},{128,160},{160,192},{192,224},{224... | collective-permute-start | bytes 417800 | tf_op jit(solution)/shard_map/ppermute | solution.py:383
  43.8 13.1 %collective-permute-start.15 = (bf16[272,256]{1,0:T(8,128)(2,1)S(1)}, bf16[272,256]{1,0:T(8,128)(2,1)S(1)}, u32[]{:S(2)}, u32[]{:S(2)}) collective-permute-start(bf16[272,256]{1,0:T(8,128)(2,1)S(1)} %collective-permute-done.14.bb), channel_id=1, source_target_pairs={{0,224},{32,0},{64,32},{96,64},{128,96},{160,128},{192,160},{224,1... | collective-permute-start | bytes 417800 | tf_op jit(solution)/shard_map/ppermute | solution.py:383
  58.2 9.3 %collective-permute-start.20 = (bf16[272,256]{1,0:T(8,128)(2,1)S(1)}, bf16[272,256]{1,0:T(8,128)(2,1)S(1)}, u32[]{:S(2)}, u32[]{:S(2)}) collective-permute-start(bf16[272,256]{1,0:T(8,128)(2,1)S(1)} %collective-permute-done.11.fb), channel_id=1, source_target_pairs={{0,32},{32,64},{64,96},{96,128},{128,160},{160,192},{192,224},{224... | collective-permute-start | bytes 417800 | tf_op jit(solution)/shard_map/ppermute | solution.py:383
  58.9 8.5 %collective-permute-start.21 = (bf16[272,256]{1,0:T(8,128)(2,1)S(1)}, bf16[272,256]{1,0:T(8,128)(2,1)S(1)}, u32[]{:S(2)}, u32[]{:S(2)}) collective-permute-start(bf16[272,256]{1,0:T(8,128)(2,1)S(1)} %collective-permute-done.13.ba), channel_id=1, source_target_pairs={{0,224},{32,0},{64,32},{96,64},{128,96},{160,128},{192,160},{224,1... | collective-permute-start | bytes 417800 | tf_op jit(solution)/shard_map/ppermute | solution.py:383
  61.4 7.6 %collective-permute-start.22 = (bf16[272,256]{1,0:T(8,128)(2,1)S(1)}, bf16[272,256]{1,0:T(8,128)(2,1)S(1)}, u32[]{:S(2)}, u32[]{:S(2)}) collective-permute-start(bf16[272,256]{1,0:T(8,128)(2,1)S(1)} %collective-permute-done.15.bb), channel_id=1, source_target_pairs={{0,224},{32,0},{64,32},{96,64},{128,96},{160,128},{192,160},{224,1... | collective-permute-start | bytes 417800 | tf_op jit(solution)/shard_map/ppermute | solution.py:383
  81.2 8.1 %collective-permute-start.25 = (f32[136,256]{1,0:T(8,128)}, f32[136,256]{1,0:T(8,128)S(1)}, u32[]{:S(2)}, u32[]{:S(2)}) collective-permute-start(f32[136,256]{1,0:T(8,128)} %get-tuple-element.89), channel_id=1, source_target_pairs={{0,16},{8,24},{16,0},{24,8},{1,17},{9,25},{17,1},{25,9},{2,18},{10... | collective-permute-start | bytes 417800 | tf_op jit(solution)/shard_map/ppermute | solution.py:379
  81.2 8.1 %collective-permute-start.26 = (f32[136,256]{1,0:T(8,128)}, f32[136,256]{1,0:T(8,128)S(1)}, u32[]{:S(2)}, u32[]{:S(2)}) collective-permute-start(f32[136,256]{1,0:T(8,128)} %get-tuple-element.90), channel_id=1, source_target_pairs={{0,8},{8,0},{16,24},{24,16},{1,9},{9,1},{17,25},{25,17},{2,10},{10... | collective-permute-start | bytes 417800 | tf_op jit(solution)/shard_map/ppermute | solution.py:379
  81.2 8.0 %collective-permute-start.27 = (f32[136,256]{1,0:T(8,128)}, f32[136,256]{1,0:T(8,128)S(1)}, u32[]{:S(2)}, u32[]{:S(2)}) collective-permute-start(f32[136,256]{1,0:T(8,128)} %get-tuple-element.91), channel_id=1, source_target_pairs={{0,24},{8,16},{16,8},{24,0},{1,25},{9,17},{17,9},{25,1},{2,26},{10... | collective-permute-start | bytes 417800 | tf_op jit(solution)/shard_map/ppermute | solution.py:379
  93.3 19.5 %all-to-all-start = ((bf16[8,256,256]{2,1,0:T(8,128)(2,1)}), bf16[8,256,256]{2,1,0:T(8,128)(2,1)S(1)}, u32[]{:S(2)}, u32[]{:S(2)}) async-start(bf16[8,256,256]{2,1,0:T(8,128)(2,1)} %merge.1), calls=%async_computation | async-start | bytes 2097152 | tf_op jit(solution)/shard_map/all_to_all | solution.py:422
  139.8 32.0 %all-to-all-start.2 = ((bf16[8,512,256]{2,1,0:T(8,128)(2,1)}), bf16[8,512,256]{2,1,0:T(8,128)(2,1)S(1)}, u32[]{:S(2)}, u32[]{:S(2)}) async-start(bf16[8,512,256]{2,1,0:T(8,128)(2,1)} %broadcast_in_dim.18), calls=%async_computation.2 | async-start | bytes 4194304 | tf_op jit(solution)/shard_map/all_to_all | solution.py:427
  147.5 7.8 %collective-permute-start.30 = (bf16[352,2048]{1,0:T(8,128)(2,1)}, bf16[352,2048]{1,0:T(8,128)(2,1)}, u32[]{:S(2)}, u32[]{:S(2)}) collective-permute-start(bf16[352,2048]{1,0:T(8,128)(2,1)} %bitcast.28), channel_id=1, source_target_pairs={{0,8},{8,0},{1,9},{9,1},{2,10},{10,2},{3,11},{11,3},{4,12},{12,4},... | collective-permute-start | bytes 4325384 | tf_op jit(solution)/shard_map/ppermute | solution.py:417
  (43 other events, 248.9 us)

commit v3 on v2

v3 whole, which is shorter than its diff:
```python
import functools
import math

import jax
import jax.numpy as jnp
import numpy as np
from jax import lax
from jax.experimental import pallas as pl
from jax.experimental.pallas import tpu as pltpu
from jax.sharding import Mesh, PartitionSpec as P

HEAD = 128
EXPERTS = 16
CAP = 32
BLK = 256
NEG = -1e30
NORM_EPS = 1e-05
SEQ = ("z", "yh", "c")
CHIPS = ("z", "yh")
TP = ("x", "yl")
SHIFTS = [(dx, dy) for dx in range(4) for dy in range(2)]
F32 = jnp.float32
BF16 = jnp.bfloat16

VMEM = pl.BlockSpec(memory_space=pltpu.VMEM)
SMEM = pl.BlockSpec(memory_space=pltpu.SMEM)


def nt_dot(a, b):
    return lax.dot_general(a, b, (((1,), (1,)), ((), ())), preferred_element_type=F32)


def tn_dot(a, b):
    return lax.dot_general(a, b, (((0,), (0,)), ((), ())), preferred_element_type=F32)


def vmem(mib):
    return pltpu.CompilerParams(vmem_limit_bytes=mib << 20)


def project(blocks, w):
    first = lax.axis_index("c") == 0
    x, yl = lax.axis_index("x"), lax.axis_index("yl")
    total = None
    for j, (dx, dy) in enumerate(SHIFTS):
        source = ((x + 4 - dx) % 4) * 2 + (yl + dy) % 2
        rows = pl.ds(pl.multiple_of(source * BLK, BLK), BLK)
        term = jnp.dot(blocks[j][...], w[rows, :], preferred_element_type=F32)
        total = term if total is None else total + term
    left, right = total[:, :HEAD], total[:, HEAD:]
    mine = jnp.where(first, left, right).astype(BF16)
    other = jnp.where(first, right, left).astype(BF16)
    return mine, other


def kv_kernel(*refs):
    blocks = refs[:8]
    wk, wv, frames, kv_own, kv_c = refs[8:]
    kv_own[:BLK, :HEAD], kv_c[:BLK, :HEAD] = project(blocks, wk)
    kv_own[:BLK, HEAD:], kv_c[:BLK, HEAD:] = project(blocks, wv)
    tail = jnp.broadcast_to(frames[...], (16, BLK)).astype(BF16)
    kv_own[BLK:, :] = tail
    kv_c[BLK:, :] = tail


def q_kernel(*refs):
    blocks = refs[:8]
    wq, frames, q_own, q_c = refs[8:]
    tail = jnp.broadcast_to(frames[...], (16, BLK)).astype(BF16)
    q_own[:BLK, :], q_c[:BLK, :] = project(blocks, wq)
    for q in (q_own, q_c):
        q[BLK : BLK + 16, :] = tail[:, :HEAD]
        q[BLK + 16 :, :] = tail[:, HEAD:]


def keys_values(blocks, wk, wv, frames):
    kv = jax.ShapeDtypeStruct((BLK + 16, 2 * HEAD), BF16)
    return pl.pallas_call(
        kv_kernel,
        out_shape=(kv, kv),
        in_specs=[VMEM] * 11,
        out_specs=(VMEM,) * 2,
        cost_estimate=pl.CostEstimate(
            flops=2 * BLK * 2048 * 512, bytes_accessed=3 << 20, transcendentals=0
        ),
        compiler_params=vmem(16),
        name="keys_values",
    )(*blocks, wk, wv, frames)


def queries(blocks, wq, frames):
    q = jax.ShapeDtypeStruct((BLK + 32, HEAD), BF16)
    return pl.pallas_call(
        q_kernel,
        out_shape=(q, q),
        in_specs=[VMEM] * 10,
        out_specs=(VMEM,) * 2,
        cost_estimate=pl.CostEstimate(
            flops=2 * BLK * 2048 * 256, bytes_accessed=2 << 20, transcendentals=0
        ),
        compiler_params=vmem(16),
        name="queries",
    )(*blocks, wq, frames)


def join_kernel(own, got, out):
    out[:BLK, :] = own[:BLK, :]
    out[BLK : 2 * BLK, :] = got[:BLK, :]
    row = lax.broadcasted_iota(jnp.int32, (16, BLK), 0)
    out[2 * BLK :, :] = jnp.where(row == 0, own[BLK:, :].astype(F32), got[BLK:, :].astype(F32)).astype(BF16)


def join(own, got):
    return pl.pallas_call(
        join_kernel,
        out_shape=jax.ShapeDtypeStruct((2 * BLK + 16, 2 * HEAD), BF16),
        in_specs=[VMEM] * 2,
        out_specs=VMEM,
        cost_estimate=pl.CostEstimate(flops=BLK * BLK, bytes_accessed=1 << 19, transcendentals=0),
        compiler_params=vmem(8),
        name="join",
    )(own, got)


def visit(q_s, f_s, m_s, l_s, acc_s, kv, masked):
    scale = 1.0 / math.sqrt(HEAD)
    s = nt_dot(kv[: 2 * BLK, :HEAD], q_s[...]) * scale
    if masked:
        lines = [jnp.broadcast_to(kv[r : r + 1, :].astype(F32), (HEAD, BLK)) for r in (2 * BLK, 2 * BLK + 1)]
        frames = jnp.concatenate([jnp.transpose(line)[:, :1] for line in lines], axis=0)
        allowed = frames <= f_s[...]
        s = jnp.where(allowed, s, NEG)
    old = m_s[...]
    top = jnp.maximum(old, jnp.max(s, axis=0, keepdims=True))
    decay = jnp.exp(old - top)
    p = jnp.exp(s - top)
    if masked:
        p = jnp.where(allowed, p, 0.0)
    m_s[...] = top
    l_s[...] = l_s[...] * decay + jnp.sum(p, axis=0, keepdims=True)
    acc_s[...] = acc_s[...] * decay + tn_dot(kv[: 2 * BLK, HEAD:], p.astype(BF16))


def local_kernel(q0, q1, q2, q3, kv, q_s, f_s, m_s, l_s, acc_s):
    for g, q in enumerate((q0, q1, q2, q3)):
        q_s[g * BLK : (g + 1) * BLK, :] = q[:BLK, :]
        for half in range(2):
            lanes = slice(g * BLK + half * HEAD, g * BLK + (half + 1) * HEAD)
            f_s[:, lanes] = q[BLK + 16 * half : BLK + 16 * half + 1, :].astype(F32)
    m_s[...] = jnp.full_like(m_s, NEG)
    l_s[...] = jnp.zeros_like(l_s)
    acc_s[...] = jnp.zeros_like(acc_s)
    visit(q_s, f_s, m_s, l_s, acc_s, kv, True)


STATE = (
    jax.ShapeDtypeStruct((4 * BLK, HEAD), BF16),
    jax.ShapeDtypeStruct((1, 4 * BLK), F32),
    jax.ShapeDtypeStruct((1, 4 * BLK), F32),
    jax.ShapeDtypeStruct((1, 4 * BLK), F32),
    jax.ShapeDtypeStruct((HEAD, 4 * BLK), F32),
)


def visit_cost(blocks):
    work = 1024 * BLK * blocks
    return pl.CostEstimate(flops=4 * work * HEAD, bytes_accessed=2 << 20, transcendentals=work)


def local(q0, q1, q2, q3, kv):
    return pl.pallas_call(
        local_kernel,
        out_shape=STATE,
        in_specs=[VMEM] * 5,
        out_specs=(VMEM,) * 5,
        cost_estimate=visit_cost(4),
        compiler_params=vmem(24),
        name="local",
    )(q0, q1, q2, q3, kv)


def step_kernel(k, q_s, f_s, m_i, l_i, acc_i, f, b, m_s, l_s, acc_s):
    z = lax.axis_index("z")
    m_s[...] = m_i[...]
    l_s[...] = l_i[...]
    acc_s[...] = acc_i[...]

    @pl.when(z >= k)
    def _():
        visit(q_s, f_s, m_s, l_s, acc_s, f, False)

    wrapped = z + k >= 8
    if k == 1:
        wrapped = wrapped | (lax.axis_index("yh") == 0)

    @pl.when(wrapped)
    def _():
        visit(q_s, f_s, m_s, l_s, acc_s, b, k == 1)


def step(k, state, f, b):
    m, l, acc = pl.pallas_call(
        functools.partial(step_kernel, k),
        out_shape=STATE[2:],
        in_specs=[VMEM] * 7,
        out_specs=(VMEM,) * 3,
        cost_estimate=visit_cost(4),
        compiler_params=vmem(24),
        name="step",
    )(*state, f, b)
    return state[0], state[1], m, l, acc


def last_kernel(q_s, f_s, m_i, l_i, acc_i, kv, o0, o1, o2, o3, m_s, l_s, acc_s):
    m_s[...] = m_i[...]
    l_s[...] = l_i[...]
    acc_s[...] = acc_i[...]

    @pl.when(lax.axis_index("z") >= 4)
    def _():
        visit(q_s, f_s, m_s, l_s, acc_s, kv, False)

    for g, out in enumerate((o0, o1, o2, o3)):
        lanes = slice(g * BLK, (g + 1) * BLK)
        total = l_s[:, lanes]
        some = total > 0.0
        safe = jnp.where(some, total, 1.0)
        out[:HEAD, :] = acc_s[:, lanes] * (1.0 / safe)
        lse = jnp.where(some, m_s[:, lanes] + jnp.log(safe), NEG)
        out[HEAD:, :] = jnp.broadcast_to(lse, (8, BLK))


def last(state, kv):
    return pl.pallas_call(
        last_kernel,
        out_shape=(jax.ShapeDtypeStruct((HEAD + 8, BLK), F32),) * 4,
        in_specs=[VMEM] * 6,
        out_specs=(VMEM,) * 4,
        scratch_shapes=[pltpu.VMEM(s.shape, s.dtype) for s in STATE[2:]],
        cost_estimate=visit_cost(2),
        compiler_params=vmem(24),
        name="last",
    )(*state, kv)


def merge_kernel(a0, a1, b0, b1, w, out):
    c = lax.axis_index("c")

    def merged(a, b):
        la, lb = a[HEAD : HEAD + 1, :], b[HEAD : HEAD + 1, :]
        top = jnp.maximum(la, lb)
        wa, wb = jnp.exp(la - top), jnp.exp(lb - top)
        inv = 1.0 / (wa + wb)
        return (a[:HEAD, :] * (wa * inv) + b[:HEAD, :] * (wb * inv)).astype(BF16)

    mine, other = merged(a0, a1), merged(b0, b1)
    rows_mine = pl.ds(pl.multiple_of(c * HEAD, HEAD), HEAD)
    rows_other = pl.ds(pl.multiple_of((1 - c) * HEAD, HEAD), HEAD)
    for t in range(8):
        cols = slice(t * BLK, (t + 1) * BLK)
        out[t] = (tn_dot(mine, w[rows_mine, cols]) + tn_dot(other, w[rows_other, cols])).astype(BF16)


def merge(a0, a1, b0, b1, w):
    return pl.pallas_call(
        merge_kernel,
        out_shape=jax.ShapeDtypeStruct((8, BLK, BLK), BF16),
        in_specs=[VMEM] * 5,
        out_specs=VMEM,
        cost_estimate=pl.CostEstimate(
            flops=2 * BLK * BLK * 2048, bytes_accessed=3 << 20, transcendentals=1024
        ),
        compiler_params=vmem(16),
        name="merge",
    )(a0, a1, b0, b1, w)


def slots_kernel(parts, stream, slot, mixed, rows):
    total = stream[...].astype(F32) + jnp.sum(parts[...].astype(F32), axis=0)
    kept = total.astype(BF16)
    mixed[...] = kept
    ids = lax.broadcasted_iota(jnp.int32, (EXPERTS * CAP, BLK), 0)
    pick = jnp.where(ids == slot[...], 1.0, 0.0).astype(BF16)
    rows[...] = jnp.dot(pick, kept, preferred_element_type=F32).astype(BF16)


def to_slots(parts, stream, slot):
    return pl.pallas_call(
        slots_kernel,
        out_shape=(
            jax.ShapeDtypeStruct((BLK, BLK), BF16),
            jax.ShapeDtypeStruct((EXPERTS * CAP, BLK), BF16),
        ),
        in_specs=[VMEM] * 3,
        out_specs=(VMEM, VMEM),
        cost_estimate=pl.CostEstimate(
            flops=2 * 512 * BLK * BLK, bytes_accessed=2 << 20, transcendentals=0
        ),
        compiler_params=vmem(16),
        name="slots",
    )(parts, stream, slot)


UNITS = 704
WIDE = 768


def pack_kernel(g0, g1, u0, u1, d0, d1, w1, w2):
    half = UNITS // 2
    pad = jnp.zeros((WIDE - UNITS, 2048), BF16)
    for w, at, a, b in ((w1, 0, g0, g1), (w1, WIDE, u0, u1), (w2, 0, d0, d1)):
        w[at : at + half, :] = a[...]
        w[at + half : at + UNITS, :] = b[...]
        w[at + UNITS : at + WIDE, :] = pad


def pack(own, far):
    return pl.pallas_call(
        pack_kernel,
        out_shape=(
            jax.ShapeDtypeStruct((2 * WIDE, 2048), BF16),
            jax.ShapeDtypeStruct((WIDE, 2048), BF16),
        ),
        in_specs=[VMEM] * 6,
        out_specs=(VMEM,) * 2,
        cost_estimate=pl.CostEstimate(flops=0, bytes_accessed=18 << 20, transcendentals=0),
        compiler_params=vmem(24),
        name="pack",
    )(own[0], far[0], own[1], far[1], own[2], far[2])


def expert_kernel(x, gain, w1_h, w2_h, out, n_s, h_s, r_s, w1, w2, sem):
    copies = [pltpu.make_async_copy(w1_h, w1, sem.at[0]), pltpu.make_async_copy(w2_h, w2, sem.at[1])]
    for copy in copies:
        copy.start()
    rows = x.shape[1]
    some = 64

    def prepare(i, carry):
        at = pl.ds(pl.multiple_of(i * some, some), some)
        square = None
        for t in range(8):
            cols = slice(t * BLK, (t + 1) * BLK)
            v = x[t, at, :].astype(F32)
            n_s[at, cols] = (v * gain[:, cols]).astype(BF16)
            square = v * v if square is None else square + v * v
        mean = jnp.sum(square, axis=1, keepdims=True) * (1.0 / 2048)
        r_s[at, :] = lax.rsqrt(mean + NORM_EPS)
        return carry

    lax.fori_loop(0, rows // some, prepare, 0)
    factor = r_s[...]
    copies[0].wait()
    for j in range(WIDE // BLK):
        cols = slice(j * BLK, (j + 1) * BLK)
        g = nt_dot(n_s[...], w1[cols, :]) * factor
        u = nt_dot(n_s[...], w1[WIDE + j * BLK : WIDE + (j + 1) * BLK, :]) * factor
        h_s[:, cols] = (g / (1.0 + jnp.exp(-g)) * u).astype(BF16)
    copies[1].wait()
    for t in range(8):
        cols = slice(t * BLK, (t + 1) * BLK)
        out[t] = jnp.dot(h_s[...], w2[:, cols], preferred_element_type=F32).astype(BF16)


def expert(x, gain, w1, w2):
    rows = x.shape[1]
    return pl.pallas_call(
        expert_kernel,
        out_shape=jax.ShapeDtypeStruct(x.shape, BF16),
        in_specs=[VMEM] * 2 + [pl.BlockSpec(memory_space=pl.ANY)] * 2,
        out_specs=VMEM,
        scratch_shapes=[
            pltpu.VMEM((rows, 2048), BF16),
            pltpu.VMEM((rows, WIDE), BF16),
            pltpu.VMEM((rows, 1), F32),
            pltpu.VMEM((2 * WIDE, 2048), BF16),
            pltpu.VMEM((WIDE, 2048), BF16),
            pltpu.SemaphoreType.DMA((2,)),
        ],
        cost_estimate=pl.CostEstimate(
            flops=6 * rows * 2048 * WIDE, bytes_accessed=13 << 20, transcendentals=rows * WIDE
        ),
        compiler_params=vmem(32),
        name="expert",
    )(x, gain, w1, w2)


def finish_kernel(mixed, rows, slot, out):
    ids = lax.broadcasted_iota(jnp.int32, (EXPERTS * CAP, BLK), 0)
    pick = jnp.where(ids == slot[...], 1.0, 0.0).astype(BF16)
    out[...] = (mixed[...].astype(F32) + tn_dot(pick, rows[...])).astype(BF16)


def finish(mixed, rows, slot):
    return pl.pallas_call(
        finish_kernel,
        out_shape=jax.ShapeDtypeStruct((BLK, BLK), BF16),
        in_specs=[VMEM] * 3,
        out_specs=VMEM,
        cost_estimate=pl.CostEstimate(
            flops=2 * 512 * BLK * BLK, bytes_accessed=1 << 20, transcendentals=0
        ),
        compiler_params=vmem(8),
        name="finish",
    )(mixed, rows, slot)


def tp_shift(a, dx, dy):
    pairs = [(i * 2 + j, ((i + dx) % 4) * 2 + (j + dy) % 2) for i in range(4) for j in range(2)]
    return lax.ppermute(a, TP, pairs)


def swap(a, dy, dc):
    pairs = [(i * 2 + j, (i ^ dy) * 2 + (j ^ dc)) for i in range(2) for j in range(2)]
    return lax.ppermute(a, ("yh", "c"), pairs)


def ring(a, step):
    return lax.ppermute(a, "z", [(i, (i + step) % 8) for i in range(8)])


def attention(blocks, wq, wk, wv, frames):
    kv_own, kv_c = keys_values(blocks, wk, wv, frames)
    kv = join(kv_own, swap(kv_c, 0, 1))
    q_own, q_c = queries(blocks, wq, frames)
    f, b = ring(kv, 1), ring(kv, -1)
    qs = (q_own, swap(q_c, 0, 1), swap(q_own, 1, 0), swap(q_c, 1, 1))
    state = local(*qs, kv)
    for k in range(1, 4):
        if k > 1:
            f, b, *state = lax.optimization_barrier((f, b, *state))
        else:
            f, b, _ = lax.optimization_barrier((f, b, q_own))
        here = f, b
        if k < 3:
            f, b = ring(f, 1), ring(b, -1)
        else:
            way = jnp.where(lax.axis_index("c") == 0, f, b)
            hops = [(i * 2 + c, (i + (-1 if c else 1)) % 8 * 2 + c) for i in range(8) for c in range(2)]
            far = lax.ppermute(way, ("z", "c"), hops)
        state = step(k, state, *here)
    return last(state, far)


def shards(stream, frames, fidelity, wq, wk, wv, wo, gain, gate, up, down):
    blocks = [stream if s == (0, 0) else tp_shift(stream, *s) for s in SHIFTS]

    route = fidelity[:, 0]
    spot = lax.iota(jnp.int32, BLK)
    same = (route[:, None] == route[None, :]) & (spot[None, :] < spot[:, None])
    slot = (route * CAP + jnp.sum(same.astype(jnp.int32), axis=1))[None, :]

    p0, p1, p2, p3 = attention(blocks, wq, wk, wv, frames[None, :])
    b0, a1, b1 = swap(p1, 0, 1), swap(p2, 1, 0), swap(p3, 1, 1)
    projected = merge(p0, a1, b0, b1, wo)

    own = (gate[0].T, up[0].T, down[0])
    *sending, projected = lax.optimization_barrier((*own, projected))
    w1, w2 = pack(own, [lax.ppermute(w, "c", [(0, 1), (1, 0)]) for w in sending])

    parts = lax.all_to_all(projected, TP, 0, 0, tiled=True)
    mixed, rows = to_slots(parts, stream, slot)
    sent = lax.all_to_all(rows.reshape(EXPERTS, CAP, BLK), CHIPS, 0, 0, tiled=True)
    sent = jnp.broadcast_to(sent.reshape(1, EXPERTS * CAP, BLK), (8, EXPERTS * CAP, BLK))
    full = lax.all_to_all(sent, TP, 0, 0, tiled=True)
    lowered = expert(full, gain[None, :], w1, w2)
    pieces = lax.all_to_all(lowered, TP, 0, 0, tiled=True)
    summed = jnp.sum(pieces.astype(F32), axis=0).astype(BF16)
    back = lax.all_to_all(summed.reshape(EXPERTS, CAP, BLK), CHIPS, 0, 0, tiled=True)
    return finish(mixed, back.reshape(EXPERTS * CAP, BLK), slot)


def solution(mesh):
    axes = ("z", "yh", "c", "x", "yl")
    fine = Mesh(np.asarray(mesh.devices).reshape(8, 2, 2, 4, 2), axes)
    return jax.shard_map(
        shards,
        mesh=fine,
        in_specs=(
            P(SEQ, TP),
            P(SEQ),
            P(SEQ, None),
            P(None, TP),
            P(None, TP),
            P(None, TP),
            P(TP, None),
            P(),
            P(SEQ, None, TP),
            P(SEQ, None, TP),
            P(SEQ, TP, None),
        ),
        out_specs=P(SEQ, TP),
        check_vma=False,
    )
```

time: 241 us -> 217 us (0.900)
  Pallas kernels: 44 us -> 15 us
  starting transfers between devices: 55.2 us -> 44.9 us
  local copies, waits for them, and re-layouts: 7.66 us -> 17.3 us
  waiting for transfers between devices: 61.8 us -> 69.2 us
    ppermute x14 -> x6, starting transfers between devices: 24.3 us -> 12.6 us  [ring(): return lax.ppermute(a, 'z', [(i, (i + step) % 8) for i in range(8)])]
    unnamed x68 -> x36, local copies, waits for them, and re-layouts: 6.19 us -> 15.9 us
    pallas_call x1, Pallas kernels: 16.7 us -> 7.28 us  [expert(): pl.pallas_call(expert_kernel, out_shape=jax.ShapeDtypeStruct(x.shape, BF1...]
    all_to_all x1, waiting for transfers between devices: 16.5 us -> 8.21 us  [shards(): full = lax.all_to_all(sent, TP, 0, 0, tiled=True)]
    pallas_call x3, Pallas kernels: 9.07 us -> 1.47 us  [step(): pl.pallas_call(functools.partial(step_kernel, k), out_shape=STATE[2:], in...]
    ppermute x3 -> x4, waiting for transfers between devices: 6.58 us -> 12.6 us  [the longest x3 6.95 us: shards(): lax.ppermute(w, 'c', [(0, 1), (1, 0)])]
    pallas_call x2 -> x5, Pallas kernels: 8.5 us -> 3.13 us  [the longest x1 1.35 us: local(): pl.pallas_call(local_kernel, out_shape=STATE, in_specs=[VMEM] * 5, out_sp...]
    ppermute x14 -> x6, waiting for transfers between devices: 8.32 us -> 13.4 us  [ring(): return lax.ppermute(a, 'z', [(i, (i + step) % 8) for i in range(8)])]
  transfers between devices with their start and end apart: 33 -> 26, of which waited for: 15 -> 19; matrix products, arithmetic and copies ran while one was open for 0% -> 0% of each run, Pallas kernels for 6% -> 2%
where the time goes in v3:
time: 217 us; the launch traced here: 215 us
  waiting for transfers between devices  69.2 us (32%)
  blocking collectives  67.5 us (31%)
  starting transfers between devices  44.9 us (21%)
  local copies, waits for them, and re-layouts  17.3 us (8%)
  Pallas kernels  15 us (7%)
    all_to_all x1, blocking collectives, shards(): pieces = lax.all_to_all(lowered, TP, 0, 0, tiled=True)  29.4 us
    all_to_all x1, blocking collectives, shards(): lax.all_to_all(rows.reshape(EXPERTS, CAP, BLK), CHIPS, 0, 0, tiled=True)  20.8 us
    all_to_all x1, blocking collectives, shards(): lax.all_to_all(summed.reshape(EXPERTS, CAP, BLK), CHIPS, 0, 0, tiled=True)  17.4 us
    unnamed x36, local copies, waits for them, and re-layouts  15.9 us
    all_to_all x1, waiting for transfers between devices, shards(): parts = lax.all_to_all(projected, TP, 0, 0, tiled=True)  15 us
    ppermute x6, waiting for transfers between devices, ring(): return lax.ppermute(a, 'z', [(i, (i + step) % 8) for i in range(8)])  13.4 us
    ppermute x6, starting transfers between devices, ring(): return lax.ppermute(a, 'z', [(i, (i + step) % 8) for i in range(8)])  12.6 us
    ppermute x7, waiting for transfers between devices, swap(): return lax.ppermute(a, ('yh', 'c'), pairs)  11 us
  transfers between devices with their start and end apart: 26, of which 19 were waited for; matrix products, arithmetic and copies ran while one was open for 0% of the time, Pallas kernels for 2%

profile of v3, /device:TPU:6, one launch (start us, length us, event | category | flops | bytes accessed | tf_op | source)
XLA Modules:
  0.0 214.7 jit_solution(6093547758319590749)
XLA Ops:
  5.6 2.4 %collective-permute-start.4 = (bf16[256,256]{1,0:T(8,128)(2,1)}, bf16[256,256]{1,0:T(8,128)(2,1)S(1)}, u32[]{:S(2)}, u32[]{:S(2)}) collective-permute-start(bf16[256,256]{1,0:T(8,128)(2,1)} %stream.1), channel_id=1, source_target_pairs={{0,5},{1,4},{2,7},{3,6},{4,1},{5,0},{6,3},{7,2},{8,13},{9,12},{10,... | collective-permute-start | bytes 393224 | tf_op jit(solution)/shard_map/ppermute | solution.py:410
  11.3 4.1 %collective-permute-done.4.refs_5_ = bf16[256,256]{1,0:T(8,128)(2,1)S(1)} collective-permute-done((bf16[256,256]{1,0:T(8,128)(2,1)}, bf16[256,256]{1,0:T(8,128)(2,1)S(1)}, u32[]{:S(2)}, u32[]{:S(2)}) %collective-permute-start.4) | collective-permute-done | bytes 131104 | tf_op jit(solution)/shard_map/ppermute | solution.py:410
  16.7 2.6 %collective-permute-done.6.refs_7_ = bf16[256,256]{1,0:T(8,128)(2,1)S(1)} collective-permute-done((bf16[256,256]{1,0:T(8,128)(2,1)}, bf16[256,256]{1,0:T(8,128)(2,1)S(1)}, u32[]{:S(2)}, u32[]{:S(2)}) %collective-permute-start.6) | collective-permute-done | bytes 131104 | tf_op jit(solution)/shard_map/ppermute | solution.py:410
  27.5 4.0 %collective-permute-start.9 = (bf16[528,256]{1,0:T(8,128)(2,1)S(1)}, bf16[528,256]{1,0:T(8,128)(2,1)S(1)}, u32[]{:S(2)}, u32[]{:S(2)}) collective-permute-start(bf16[528,256]{1,0:T(8,128)(2,1)S(1)} %join.1.kv), channel_id=1, source_target_pairs={{0,224},{32,0},{64,32},{96,64},{128,96},{160,128},{192,160},{224,1... | collective-permute-start | bytes 811016 | tf_op jit(solution)/shard_map/ppermute | solution.py:419
  32.0 6.2 %collective-permute-done.8.f = bf16[528,256]{1,0:T(8,128)(2,1)S(1)} collective-permute-done((bf16[528,256]{1,0:T(8,128)(2,1)S(1)}, bf16[528,256]{1,0:T(8,128)(2,1)S(1)}, u32[]{:S(2)}, u32[]{:S(2)}) %collective-permute-start.8) | collective-permute-done | bytes 270368 | tf_op jit(solution)/shard_map/ppermute | solution.py:419
  38.3 3.2 %collective-permute-start.11 = (bf16[528,256]{1,0:T(8,128)(2,1)S(1)}, bf16[528,256]{1,0:T(8,128)(2,1)S(1)}, u32[]{:S(2)}, u32[]{:S(2)}) collective-permute-start(bf16[528,256]{1,0:T(8,128)(2,1)S(1)} %collective-permute-done.9.b), channel_id=1, source_target_pairs={{0,224},{32,0},{64,32},{96,64},{128,96},{160,128},{192,160},{224,1... | collective-permute-start | bytes 811016 | tf_op jit(solution)/shard_map/ppermute | solution.py:419
  41.5 3.1 %collective-permute-start.13 = (bf16[288,128]{1,0:T(8,128)(2,1)S(1)}, bf16[288,128]{1,0:T(8,128)(2,1)S(1)}, u32[]{:S(2)}, u32[]{:S(2)}) collective-permute-start(bf16[288,128]{1,0:T(8,128)(2,1)S(1)} %get-tuple-element.53.q0), channel_id=1, source_target_pairs={{0,16},{8,24},{16,0},{24,8},{1,17},{9,25},{17,1},{25,9},{2,18},{10... | collective-permute-start | bytes 221192 | tf_op jit(solution)/shard_map/ppermute | solution.py:415
  47.4 2.7 %collective-permute-done.14.q3 = bf16[288,128]{1,0:T(8,128)(2,1)S(1)} collective-permute-done((bf16[288,128]{1,0:T(8,128)(2,1)S(1)}, bf16[288,128]{1,0:T(8,128)(2,1)S(1)}, u32[]{:S(2)}, u32[]{:S(2)}) %collective-permute-start.14) | collective-permute-done | bytes 73760 | tf_op jit(solution)/shard_map/ppermute | solution.py:415
  53.6 2.6 %collective-permute-start.16 = (bf16[528,256]{1,0:T(8,128)(2,1)S(1)}, bf16[528,256]{1,0:T(8,128)(2,1)S(1)}, u32[]{:S(2)}, u32[]{:S(2)}) collective-permute-start(bf16[528,256]{1,0:T(8,128)(2,1)S(1)} %collective-permute-done.11.b), channel_id=1, source_target_pairs={{0,224},{32,0},{64,32},{96,64},{128,96},{160,128},{192,160},{224,1... | collective-permute-start | bytes 811016 | tf_op jit(solution)/shard_map/ppermute | solution.py:419
  56.2 6.8 %collective-permute-done.15.f = bf16[528,256]{1,0:T(8,128)(2,1)S(1)} collective-permute-done((bf16[528,256]{1,0:T(8,128)(2,1)S(1)}, bf16[528,256]{1,0:T(8,128)(2,1)S(1)}, u32[]{:S(2)}, u32[]{:S(2)}) %collective-permute-start.15) | collective-permute-done | bytes 270368 | tf_op jit(solution)/shard_map/ppermute | solution.py:419
  65.5 5.6 %collective-permute-done.17.kv = bf16[528,256]{1,0:T(8,128)(2,1)S(1)} collective-permute-done((bf16[528,256]{1,0:T(8,128)(2,1)S(1)}, bf16[528,256]{1,0:T(8,128)(2,1)S(1)}, u32[]{:S(2)}, u32[]{:S(2)}) %collective-permute-start.17) | collective-permute-done | bytes 270368 | tf_op jit(solution)/shard_map/ppermute | solution.py:440
  72.2 2.8 %collective-permute-start.20 = (f32[136,256]{1,0:T(8,128)S(1)}, f32[136,256]{1,0:T(8,128)S(1)}, u32[]{:S(2)}, u32[]{:S(2)}) collective-permute-start(f32[136,256]{1,0:T(8,128)S(1)} %get-tuple-element.88), channel_id=1, source_target_pairs={{0,24},{8,16},{16,8},{24,0},{1,25},{9,17},{17,9},{25,1},{2,26},{10... | collective-permute-start | bytes 417800 | tf_op jit(solution)/shard_map/ppermute | solution.py:415
  75.0 4.1 %collective-permute-done.18.a1 = f32[136,256]{1,0:T(8,128)S(1)} collective-permute-done((f32[136,256]{1,0:T(8,128)S(1)}, f32[136,256]{1,0:T(8,128)S(1)}, u32[]{:S(2)}, u32[]{:S(2)}) %collective-permute-start.18) | collective-permute-done | bytes 139296 | tf_op jit(solution)/shard_map/ppermute | solution.py:415
  81.4 4.5 %all-to-all-start = ((bf16[8,256,256]{2,1,0:T(8,128)(2,1)}), bf16[8,256,256]{2,1,0:T(8,128)(2,1)S(1)}, u32[]{:S(2)}, u32[]{:S(2)}) async-start(bf16[8,256,256]{2,1,0:T(8,128)(2,1)} %merge.1), calls=%async_computation | async-start | bytes 2097152 | tf_op jit(solution)/shard_map/all_to_all | solution.py:461
  86.1 15.0 %all-to-all-done.parts = bf16[8,256,256]{2,1,0:T(8,128)(2,1)S(1)} async-done(((bf16[8,256,256]{2,1,0:T(8,128)(2,1)}), bf16[8,256,256]{2,1,0:T(8,128)(2,1)S(1)}, u32[]{:S(2)}, u32[]{:S(2)}) %all-to-all-start) | async-done | bytes 1048608 | tf_op jit(solution)/shard_map/all_to_all | solution.py:461
  101.5 20.8 %all_to_all.25 = bf16[16,32,256]{2,1,0:T(8,128)(2,1)S(1)} all-to-all(bf16[16,32,256]{2,1,0:T(8,128)(2,1)S(1)} %bitcast.24), channel_id=1, replica_groups=mesh['z'=8,'yh'=2,'c'=2,'x'=4,'yl'=2] {'z','yh'}, dimensions={0} | all-to-all | bytes 524288 | tf_op jit(solution)/shard_map/all_to_all | solution.py:463
  123.8 7.4 %all-to-all-start.2 = ((bf16[8,512,256]{2,1,0:T(8,128)(2,1)}), bf16[8,512,256]{2,1,0:T(8,128)(2,1)S(1)}, u32[]{:S(2)}, u32[]{:S(2)}) async-start(bf16[8,512,256]{2,1,0:T(8,128)(2,1)} %broadcast_in_dim.18), calls=%async_computation.2 | async-start | bytes 4194304 | tf_op jit(solution)/shard_map/all_to_all | solution.py:465
  131.8 3.8 %collective-permute-done.21.g1 = bf16[352,2048]{1,0:T(8,128)(2,1)S(1)} collective-permute-done((bf16[352,2048]{1,0:T(8,128)(2,1)S(1)}, bf16[352,2048]{1,0:T(8,128)(2,1)S(1)}, u32[]{:S(2)}, u32[]{:S(2)}) %collective-permute-start.21) | collective-permute-done | bytes 1441824 | tf_op jit(solution)/shard_map/ppermute | solution.py:459
  142.1 2.7 %copy-done.12 = bf16[1536,2048]{1,0:T(8,128)(2,1)} copy-done((bf16[1536,2048]{1,0:T(8,128)(2,1)}, bf16[1536,2048]{1,0:T(8,128)(2,1)S(1)}, u32[]{:S(2)}) %copy-start.12) | copy-done | bytes 6291480
  146.5 8.2 %all-to-all-done.2.x = bf16[8,512,256]{2,1,0:T(8,128)(2,1)S(1)} async-done(((bf16[8,512,256]{2,1,0:T(8,128)(2,1)}), bf16[8,512,256]{2,1,0:T(8,128)(2,1)S(1)}, u32[]{:S(2)}, u32[]{:S(2)}) %all-to-all-start.2) | async-done | bytes 2097184 | tf_op jit(solution)/shard_map/all_to_all | solution.py:465
  154.7 2.8 %copy-done.13 = bf16[1536,2048]{1,0:T(8,128)(2,1)S(1)} copy-done((bf16[1536,2048]{1,0:T(8,128)(2,1)S(1)}, bf16[1536,2048]{1,0:T(8,128)(2,1)}, u32[]{:S(2)}) %copy-start.13) | copy-done | bytes 6291480
  159.4 7.3 %expert.1 = bf16[8,512,256]{2,1,0:T(8,128)(2,1)S(1)} custom-call(bf16[8,512,256]{2,1,0:T(8,128)(2,1)S(1)} %all-to-all-done.2.x, f32[1,2048]{1,0:T(1,128)S(1)} %bitcast.27, bf16[1536,2048]{1,0:T(8,128)(2,1)S(1)} %copy-done.13, bf16[768,2048]{1,0:T(8,128)(2,1)S(1)} %copy-done.15), custom_call_target="tpu_custom_call" | custom-call | flops 4831838208 | bytes 13631488 | tf_op jit(solution)/shard_map/expert/pallas_call | solution.py:367
  166.7 29.4 %all_to_all.26 = bf16[8,512,256]{2,1,0:T(8,128)(2,1)S(1)} all-to-all(bf16[8,512,256]{2,1,0:T(8,128)(2,1)S(1)} %expert.1), channel_id=1, replica_groups=mesh['z'=8,'yh'=2,'c'=2,'x'=4,'yl'=2] {'x','yl'}, dimensions={0} | all-to-all | bytes 4194304 | tf_op jit(solution)/shard_map/all_to_all | solution.py:467
  196.4 17.4 %all_to_all.27 = bf16[16,32,256]{2,1,0:T(8,128)(2,1)S(1)} all-to-all(bf16[16,32,256]{2,1,0:T(8,128)(2,1)S(1)} %bitcast.28), channel_id=1, replica_groups=mesh['z'=8,'yh'=2,'c'=2,'x'=4,'yl'=2] {'z','yh'}, dimensions={0} | all-to-all | bytes 524288 | tf_op jit(solution)/shard_map/all_to_all | solution.py:469
  (85 shorter events, 45.0 us)
Async XLA Ops:
  0.0 8.0 %collective-permute-start = (bf16[256,256]{1,0:T(8,128)(2,1)}, bf16[256,256]{1,0:T(8,128)(2,1)S(1)}, u32[]{:S(2)}, u32[]{:S(2)}) collective-permute-start(bf16[256,256]{1,0:T(8,128)(2,1)} %stream.1), channel_id=1, source_target_pairs={{0,1},{1,0},{2,3},{3,2},{4,5},{5,4},{6,7},{7,6},{8,9},{9,8},{10,11... | collective-permute-start | bytes 393224 | tf_op jit(solution)/shard_map/ppermute | solution.py:410
  1.6 7.1 %collective-permute-start.1 = (bf16[256,256]{1,0:T(8,128)(2,1)}, bf16[256,256]{1,0:T(8,128)(2,1)S(1)}, u32[]{:S(2)}, u32[]{:S(2)}) collective-permute-start(bf16[256,256]{1,0:T(8,128)(2,1)} %stream.1), channel_id=1, source_target_pairs={{0,2},{1,3},{2,4},{3,5},{4,6},{5,7},{6,0},{7,1},{8,10},{9,11},{10,... | collective-permute-start | bytes 393224 | tf_op jit(solution)/shard_map/ppermute | solution.py:410
  2.2 8.8 %collective-permute-start.2 = (bf16[256,256]{1,0:T(8,128)(2,1)}, bf16[256,256]{1,0:T(8,128)(2,1)S(1)}, u32[]{:S(2)}, u32[]{:S(2)}) collective-permute-start(bf16[256,256]{1,0:T(8,128)(2,1)} %stream.1), channel_id=1, source_target_pairs={{0,3},{1,2},{2,5},{3,4},{4,7},{5,6},{6,1},{7,0},{8,11},{9,10},{10,... | collective-permute-start | bytes 393224 | tf_op jit(solution)/shard_map/ppermute | solution.py:410
  3.7 7.6 %collective-permute-start.3 = (bf16[256,256]{1,0:T(8,128)(2,1)}, bf16[256,256]{1,0:T(8,128)(2,1)S(1)}, u32[]{:S(2)}, u32[]{:S(2)}) collective-permute-start(bf16[256,256]{1,0:T(8,128)(2,1)} %stream.1), channel_id=1, source_target_pairs={{0,4},{1,5},{2,6},{3,7},{4,0},{5,1},{6,2},{7,3},{8,12},{9,13},{10,... | collective-permute-start | bytes 393224 | tf_op jit(solution)/shard_map/ppermute | solution.py:410
  5.6 9.8 %collective-permute-start.4 = (bf16[256,256]{1,0:T(8,128)(2,1)}, bf16[256,256]{1,0:T(8,128)(2,1)S(1)}, u32[]{:S(2)}, u32[]{:S(2)}) collective-permute-start(bf16[256,256]{1,0:T(8,128)(2,1)} %stream.1), channel_id=1, source_target_pairs={{0,5},{1,4},{2,7},{3,6},{4,1},{5,0},{6,3},{7,2},{8,13},{9,12},{10,... | collective-permute-start | bytes 393224 | tf_op jit(solution)/shard_map/ppermute | solution.py:410
  8.0 8.7 %collective-permute-start.5 = (bf16[256,256]{1,0:T(8,128)(2,1)}, bf16[256,256]{1,0:T(8,128)(2,1)S(1)}, u32[]{:S(2)}, u32[]{:S(2)}) collective-permute-start(bf16[256,256]{1,0:T(8,128)(2,1)} %stream.1), channel_id=1, source_target_pairs={{0,6},{1,7},{2,0},{3,1},{4,2},{5,3},{6,4},{7,5},{8,14},{9,15},{10,... | collective-permute-start | bytes 393224 | tf_op jit(solution)/shard_map/ppermute | solution.py:410
  8.7 10.6 %collective-permute-start.6 = (bf16[256,256]{1,0:T(8,128)(2,1)}, bf16[256,256]{1,0:T(8,128)(2,1)S(1)}, u32[]{:S(2)}, u32[]{:S(2)}) collective-permute-start(bf16[256,256]{1,0:T(8,128)(2,1)} %stream.1), channel_id=1, source_target_pairs={{0,7},{1,6},{2,1},{3,0},{4,3},{5,2},{6,5},{7,4},{8,15},{9,14},{10,... | collective-permute-start | bytes 393224 | tf_op jit(solution)/shard_map/ppermute | solution.py:410
  25.5 12.7 %collective-permute-start.8 = (bf16[528,256]{1,0:T(8,128)(2,1)S(1)}, bf16[528,256]{1,0:T(8,128)(2,1)S(1)}, u32[]{:S(2)}, u32[]{:S(2)}) collective-permute-start(bf16[528,256]{1,0:T(8,128)(2,1)S(1)} %join.1.kv), channel_id=1, source_target_pairs={{0,32},{32,64},{64,96},{96,128},{128,160},{160,192},{192,224},{224... | collective-permute-start | bytes 811016 | tf_op jit(solution)/shard_map/ppermute | solution.py:419
  27.5 10.7 %collective-permute-start.9 = (bf16[528,256]{1,0:T(8,128)(2,1)S(1)}, bf16[528,256]{1,0:T(8,128)(2,1)S(1)}, u32[]{:S(2)}, u32[]{:S(2)}) collective-permute-start(bf16[528,256]{1,0:T(8,128)(2,1)S(1)} %join.1.kv), channel_id=1, source_target_pairs={{0,224},{32,0},{64,32},{96,64},{128,96},{160,128},{192,160},{224,1... | collective-permute-start | bytes 811016 | tf_op jit(solution)/shard_map/ppermute | solution.py:419
  38.3 14.6 %collective-permute-start.10 = (bf16[528,256]{1,0:T(8,128)(2,1)S(1)}, bf16[528,256]{1,0:T(8,128)(2,1)S(1)}, u32[]{:S(2)}, u32[]{:S(2)}) collective-permute-start(bf16[528,256]{1,0:T(8,128)(2,1)S(1)} %collective-permute-done.8.f), channel_id=1, source_target_pairs={{0,32},{32,64},{64,96},{96,128},{128,160},{160,192},{192,224},{224... | collective-permute-start | bytes 811016 | tf_op jit(solution)/shard_map/ppermute | solution.py:419
  38.3 14.6 %collective-permute-start.11 = (bf16[528,256]{1,0:T(8,128)(2,1)S(1)}, bf16[528,256]{1,0:T(8,128)(2,1)S(1)}, u32[]{:S(2)}, u32[]{:S(2)}) collective-permute-start(bf16[528,256]{1,0:T(8,128)(2,1)S(1)} %collective-permute-done.9.b), channel_id=1, source_target_pairs={{0,224},{32,0},{64,32},{96,64},{128,96},{160,128},{192,160},{224,1... | collective-permute-start | bytes 811016 | tf_op jit(solution)/shard_map/ppermute | solution.py:419
  41.5 5.9 %collective-permute-start.13 = (bf16[288,128]{1,0:T(8,128)(2,1)S(1)}, bf16[288,128]{1,0:T(8,128)(2,1)S(1)}, u32[]{:S(2)}, u32[]{:S(2)}) collective-permute-start(bf16[288,128]{1,0:T(8,128)(2,1)S(1)} %get-tuple-element.53.q0), channel_id=1, source_target_pairs={{0,16},{8,24},{16,0},{24,8},{1,17},{9,25},{17,1},{25,9},{2,18},{10... | collective-permute-start | bytes 221192 | tf_op jit(solution)/shard_map/ppermute | solution.py:415
  44.7 5.4 %collective-permute-start.14 = (bf16[288,128]{1,0:T(8,128)(2,1)S(1)}, bf16[288,128]{1,0:T(8,128)(2,1)S(1)}, u32[]{:S(2)}, u32[]{:S(2)}) collective-permute-start(bf16[288,128]{1,0:T(8,128)(2,1)S(1)} %get-tuple-element.56), channel_id=1, source_target_pairs={{0,24},{8,16},{16,8},{24,0},{1,25},{9,17},{17,9},{25,1},{2,26},{10... | collective-permute-start | bytes 221192 | tf_op jit(solution)/shard_map/ppermute | solution.py:415
  52.9 10.2 %collective-permute-start.15 = (bf16[528,256]{1,0:T(8,128)(2,1)S(1)}, bf16[528,256]{1,0:T(8,128)(2,1)S(1)}, u32[]{:S(2)}, u32[]{:S(2)}) collective-permute-start(bf16[528,256]{1,0:T(8,128)(2,1)S(1)} %collective-permute-done.10.f), channel_id=1, source_target_pairs={{0,32},{32,64},{64,96},{96,128},{128,160},{160,192},{192,224},{224... | collective-permute-start | bytes 811016 | tf_op jit(solution)/shard_map/ppermute | solution.py:419
  53.6 9.8 %collective-permute-start.16 = (bf16[528,256]{1,0:T(8,128)(2,1)S(1)}, bf16[528,256]{1,0:T(8,128)(2,1)S(1)}, u32[]{:S(2)}, u32[]{:S(2)}) collective-permute-start(bf16[528,256]{1,0:T(8,128)(2,1)S(1)} %collective-permute-done.11.b), channel_id=1, source_target_pairs={{0,224},{32,0},{64,32},{96,64},{128,96},{160,128},{192,160},{224,1... | collective-permute-start | bytes 811016 | tf_op jit(solution)/shard_map/ppermute | solution.py:419
  63.4 7.7 %collective-permute-start.17 = (bf16[528,256]{1,0:T(8,128)(2,1)S(1)}, bf16[528,256]{1,0:T(8,128)(2,1)S(1)}, u32[]{:S(2)}, u32[]{:S(2)}) collective-permute-start(bf16[528,256]{1,0:T(8,128)(2,1)S(1)} %broadcast_select_fusion), channel_id=1, source_target_pairs={{0,32},{8,232},{32,64},{40,8},{64,96},{72,40},{96,128},{104,72},{1... | collective-permute-start | bytes 811016 | tf_op jit(solution)/shard_map/ppermute | solution.py:440
  71.2 7.9 %collective-permute-start.18 = (f32[136,256]{1,0:T(8,128)S(1)}, f32[136,256]{1,0:T(8,128)S(1)}, u32[]{:S(2)}, u32[]{:S(2)}) collective-permute-start(f32[136,256]{1,0:T(8,128)S(1)} %get-tuple-element.86), channel_id=1, source_target_pairs={{0,16},{8,24},{16,0},{24,8},{1,17},{9,25},{17,1},{25,9},{2,18},{10... | collective-permute-start | bytes 417800 | tf_op jit(solution)/shard_map/ppermute | solution.py:415
  72.2 6.9 %collective-permute-start.19 = (f32[136,256]{1,0:T(8,128)S(1)}, f32[136,256]{1,0:T(8,128)S(1)}, u32[]{:S(2)}, u32[]{:S(2)}) collective-permute-start(f32[136,256]{1,0:T(8,128)S(1)} %get-tuple-element.87), channel_id=1, source_target_pairs={{0,8},{8,0},{16,24},{24,16},{1,9},{9,1},{17,25},{25,17},{2,10},{10... | collective-permute-start | bytes 417800 | tf_op jit(solution)/shard_map/ppermute | solution.py:415
  72.2 7.5 %collective-permute-start.20 = (f32[136,256]{1,0:T(8,128)S(1)}, f32[136,256]{1,0:T(8,128)S(1)}, u32[]{:S(2)}, u32[]{:S(2)}) collective-permute-start(f32[136,256]{1,0:T(8,128)S(1)} %get-tuple-element.88), channel_id=1, source_target_pairs={{0,24},{8,16},{16,8},{24,0},{1,25},{9,17},{17,9},{25,1},{2,26},{10... | collective-permute-start | bytes 417800 | tf_op jit(solution)/shard_map/ppermute | solution.py:415
  81.4 19.7 %all-to-all-start = ((bf16[8,256,256]{2,1,0:T(8,128)(2,1)}), bf16[8,256,256]{2,1,0:T(8,128)(2,1)S(1)}, u32[]{:S(2)}, u32[]{:S(2)}) async-start(bf16[8,256,256]{2,1,0:T(8,128)(2,1)} %merge.1), calls=%async_computation | async-start | bytes 2097152 | tf_op jit(solution)/shard_map/all_to_all | solution.py:461
  123.8 30.9 %all-to-all-start.2 = ((bf16[8,512,256]{2,1,0:T(8,128)(2,1)}), bf16[8,512,256]{2,1,0:T(8,128)(2,1)S(1)}, u32[]{:S(2)}, u32[]{:S(2)}) async-start(bf16[8,512,256]{2,1,0:T(8,128)(2,1)} %broadcast_in_dim.18), calls=%async_computation.2 | async-start | bytes 4194304 | tf_op jit(solution)/shard_map/all_to_all | solution.py:465
  131.2 4.4 %collective-permute-start.21 = (bf16[352,2048]{1,0:T(8,128)(2,1)S(1)}, bf16[352,2048]{1,0:T(8,128)(2,1)S(1)}, u32[]{:S(2)}, u32[]{:S(2)}) collective-permute-start(bf16[352,2048]{1,0:T(8,128)(2,1)S(1)} %bitcast.17), channel_id=1, source_target_pairs={{0,8},{8,0},{1,9},{9,1},{2,10},{10,2},{3,11},{11,3},{4,12},{12,4},... | collective-permute-start | bytes 4325384 | tf_op jit(solution)/shard_map/ppermute | solution.py:459
  131.2 5.5 %collective-permute-start.22 = (bf16[352,2048]{1,0:T(8,128)(2,1)}, bf16[352,2048]{1,0:T(8,128)(2,1)S(1)}, u32[]{:S(2)}, u32[]{:S(2)}) collective-permute-start(bf16[352,2048]{1,0:T(8,128)(2,1)} %bitcast.19), channel_id=1, source_target_pairs={{0,8},{8,0},{1,9},{9,1},{2,10},{10,2},{3,11},{11,3},{4,12},{12,4},... | collective-permute-start | bytes 4325384 | tf_op jit(solution)/shard_map/ppermute | solution.py:459
  131.7 7.0 %collective-permute-start.23 = (bf16[352,2048]{1,0:T(8,128)(2,1)}, bf16[352,2048]{1,0:T(8,128)(2,1)S(1)}, u32[]{:S(2)}, u32[]{:S(2)}) collective-permute-start(bf16[352,2048]{1,0:T(8,128)(2,1)} %bitcast.21), channel_id=1, source_target_pairs={{0,8},{8,0},{1,9},{9,1},{2,10},{10,2},{3,11},{11,3},{4,12},{12,4},... | collective-permute-start | bytes 4325384 | tf_op jit(solution)/shard_map/ppermute | solution.py:459
  (20 other events, 156.3 us)
